TPU v7x, 128 devices: a whole 4x4x4 slice. The times are simulated.
128 devices in a mesh: bulk: 8 (over y, core), front: 16 (over x, z).
Axes of the slice: x: 4, y: 4, z: 4, core: 2. Of those that a mesh axis runs over, the one named last changes fastest.
Arguments:
- child_pivot: float32 [8, 2048, 2048], P('bulk', 'front'), may hold values from -20 to 40, as said below
- child_coupling: float32 [8, 2048, 2048], P('bulk', 'front'), may hold values from -0.75 to 0.75
- parent_arrow: float32 [8192, 1024], P(('bulk', 'front')), may hold values from -600 to 3000, as said below
- row_map: int32 [8, 2048], P('bulk', 'front'), may hold values from 0 to 8191, as said below
- block_pattern: int32 [64, 8], replicated, may hold values from 0 to 1, as said below
Outputs:
- child_factor_pivot: float32 [8, 2048, 2048], P('bulk', 'front')
- child_factor_coupling: float32 [8, 2048, 2048], P('bulk', 'front')
- parent_factor: float32 [8192, 1024], P(('bulk', 'front'))
Inputs may be any that keep to these rules, and one draw needn't show every extreme that they name: `child_pivot`: each child's matrix is symmetric and positive definite. `parent_arrow`: the first 1024 rows hold a symmetric block that stays positive definite when contribution is added. `row_map`: A child's 2048 entries are distinct. Entry i of a child names a row r with (r // 64) % (16) == i // 128. `block_pattern`: every block (i, i) with i < 8 is 1.
All inputs are finite; a program needn't handle non-finite values.
Results may differ from a plain program's by a relative error of at most 0.00022.
Values sent between devices are 32-bit elements; how exact they have to be, the bound alone decides.
A program may use at most 128 MiB of HBM per device.

v0:
```python
import jax
import jax.numpy as jnp
from jax import lax
from jax.sharding import PartitionSpec as P

BLOCK = 128
PANEL = 512


HIGHEST_PRECISION = lax.Precision.HIGHEST


def rows_for(lines, devices):
    spare = -len(lines) % devices
    return jnp.pad(lines, [(0, spare)] + [(0, 0)] * (lines.ndim - 1))


def from_root(array, axis, root):
    lines = jnp.where(lax.axis_index(axis) == root, array, jnp.zeros_like(array)).reshape(
        -1, *array.shape[1:][-1:]
    )
    padded = rows_for(lines, lax.axis_size(axis))
    own = lax.psum_scatter(padded, axis, scatter_dimension=0, tiled=True)
    return lax.all_gather(own, axis, axis=0, tiled=True)[: len(lines)].reshape(array.shape)


def cut_along(array, dim, devices):
    before, after = (array.shape[:dim], array.shape[dim + 1 :])
    return jnp.moveaxis(array.reshape(*before, devices, -1, *after), dim, 0)


def sent_and_summed(array, axis, dim):
    pieces = cut_along(array, dim, lax.axis_size(axis))
    arrived = lax.all_to_all(pieces, axis, split_axis=0, concat_axis=0, tiled=True)
    return arrived.sum(axis=0)


def mirror_lower(matrix):
    return jnp.tril(matrix) + jnp.tril(matrix, -1).T


def solve_right(lower_factor, matrix):
    return jax.scipy.linalg.solve_triangular(lower_factor, matrix.T, lower=True).T


def child_chain(own_rows, coupling, panel_width):
    row_count, total_cols = own_rows.shape
    first_row = lax.axis_index("front") * row_count
    global_rows = first_row + jnp.arange(row_count)
    row_ids = jnp.arange(total_cols)
    step_count = total_cols // panel_width

    def advance(step_now, carried):
        own_state, coupling_state = carried
        col_start = step_now * panel_width
        column = lax.dynamic_slice_in_dim(own_state, col_start, panel_width, 1)
        gathered = lax.all_gather(column, "front", axis=0, tiled=True)
        diag_block = lax.dynamic_slice_in_dim(gathered, col_start, panel_width, 0)
        factor = jnp.linalg.cholesky(mirror_lower(diag_block))
        solved = jnp.where((row_ids >= col_start)[:, None], solve_right(factor, gathered), 0.0)
        solved = lax.dynamic_update_slice_in_dim(solved, factor, col_start, 0)
        trailing = jnp.where((row_ids >= col_start + panel_width)[:, None], solved, 0.0)
        own_factor = lax.dynamic_slice_in_dim(solved, first_row, row_count, 0)
        own_state = own_state - jnp.dot(own_factor, trailing.T, precision=HIGHEST_PRECISION)
        kept_block = lax.dynamic_slice_in_dim(own_state, col_start, panel_width, 1)
        new_block = jnp.where((global_rows >= col_start)[:, None], own_factor, kept_block)
        own_state = lax.dynamic_update_slice_in_dim(own_state, new_block, col_start, 1)
        block_part = lax.dynamic_slice_in_dim(coupling_state, col_start, panel_width, 1)
        block_part = solve_right(factor, block_part)
        coupling_state = coupling_state - jnp.dot(
            block_part, trailing.T, precision=HIGHEST_PRECISION
        )
        coupling_state = lax.dynamic_update_slice_in_dim(coupling_state, block_part, col_start, 1)
        return (own_state, coupling_state)

    own_rows, coupling = lax.fori_loop(0, step_count, advance, (own_rows, coupling))
    own_rows = jnp.where(row_ids[None, :] <= global_rows[:, None], own_rows, 0.0)
    return (own_rows, coupling)


def parent_whole(assembled, first_row, pivots):
    row_count = assembled.shape[0]
    group_rows = lax.all_gather(assembled, "front", axis=0, tiled=True)
    pivot_block = from_root(group_rows, "bulk", 0)
    factor = jnp.linalg.cholesky(mirror_lower(pivot_block))
    pivot_factor = lax.dynamic_slice_in_dim(
        factor, jnp.minimum(first_row, pivots - row_count), row_count, 0
    )
    return jnp.where(first_row < pivots, pivot_factor, solve_right(factor, assembled))


def on_device(child_pivot, child_coupling, parent_arrow, row_map, block_pattern):
    own_rows = child_pivot[0]
    coupling_rows = child_coupling[0]
    parent_index = row_map[0]
    panel_width = PANEL
    lower_rows, coupling = child_chain(own_rows, coupling_rows, panel_width)
    parent_count, pivots = parent_arrow.shape
    front_index = lax.axis_index("front")
    front_groups = lax.axis_size("front")
    local_slot = parent_index - front_index * parent_count
    landing_hits = (local_slot[:, None] == jnp.arange(parent_count)[None, :]).astype(jnp.float32)
    landing_piece = jnp.dot(landing_hits.T, coupling, precision=HIGHEST_PRECISION)
    reached = -jnp.dot(
        coupling,
        lax.all_gather(landing_piece, "front", axis=0, tiled=True).T,
        precision=HIGHEST_PRECISION,
    )
    slot_index = (
        parent_index // parent_count // front_groups * parent_count + parent_index % parent_count
    )
    spread_rows = lax.axis_size("bulk") * parent_count
    routing = (slot_index[:, None] == jnp.arange(spread_rows)[None, :]).astype(jnp.float32)
    added = sent_and_summed(jnp.dot(routing.T, reached, precision=HIGHEST_PRECISION), "bulk", 0)
    device_index = lax.axis_index("bulk") * front_groups + front_index
    first_row = device_index * parent_count
    block_rows = (first_row + jnp.arange(parent_count)) // BLOCK
    block_count = block_pattern.shape[0]
    picker = (block_rows[:, None] == jnp.arange(block_count)[None, :]).astype(jnp.float32)
    row_mask = jnp.dot(picker, block_pattern.astype(jnp.float32), precision=HIGHEST_PRECISION)
    full_mask = jnp.repeat(row_mask, BLOCK, axis=1)
    assembled = parent_arrow * full_mask + added
    parent_rows = parent_whole(assembled, first_row, pivots)
    return (lower_rows[None], coupling[None], parent_rows)


def solution(mesh):
    placed = (
        P("bulk", "front", None),
        P("bulk", "front", None),
        P(("bulk", "front"), None),
        P("bulk", "front"),
        P(),
    )
    return jax.shard_map(
        on_device,
        mesh=mesh,
        in_specs=placed,
        out_specs=(P("bulk", "front", None), P("bulk", "front", None), P(("bulk", "front"), None)),
        check_vma=False,
    )
```

profile of v0, /device:TPU:1, one launch (start us, length us, event | category | flops | bytes accessed | tf_op | source)
XLA Modules:
  0.0 1593.0 jit_solution(16100741351400434337)
XLA Ops:
  12.6 978.3 %while.26 = (s32[]{:T(128)}, f32[128,2048]{1,0:T(8,128)}, f32[128,2048]{1,0:T(8,128)}, s32[]{:T(128)}, s32[]{:T(128)}, /*index=5*/s32[]{:T(128)}, s32[]{:T(128)}...) while((s32[]{:T(128)}, f32[128,2048]{1,0:T(8,128)}, f32[128,2048]{1,0:T(8,128)}, ...), condition=%wide.region_9.13_spmd.clone.clone, body=%wide.region_0.12_spmd.clone.clone.sunk | while | flops 7915688960 | bytes 120475856 | solution.py:76
  18.8 52.0 %all-gather.11.cloned.1.call-done = f32[2048,512]{1,0:T(8,128)} async-done(((f32[128,512]{1,0:T(8,128)}), f32[2048,512]{1,0:T(8,128)}) %all-gather.11.cloned.1.call-update) | async-done | bytes 4194320 | tf_op jit(solution)/shard_map/while/body/eval_jaxpr/all_gather | solution.py:57
  74.6 11.7 cholesky.1240
  96.9 11.7 cholesky.1243
  108.7 10.2 custom-call.138
  119.6 11.7 cholesky.1245
  141.7 11.8 cholesky.1246
  159.5 10.6 while.27
  170.1 40.2 %custom-call.141 = f32[4,128,128]{1,2,0:T(8,128)S(1)} custom-call(f32[4,128,128]{2,1,0:T(8,128)} %get-tuple-element.446), custom_call_target="InvertDiagBlocksLowerTriangular" | custom-call | tf_op jit(solution)/shard_map/while/body/eval_jaxpr/jit(_solve_triangular)/triangular_solve | solution.py:43
  264.6 48.6 %all-gather.11.cloned.1.call-done = f32[2048,512]{1,0:T(8,128)} async-done(((f32[128,512]{1,0:T(8,128)}), f32[2048,512]{1,0:T(8,128)}) %all-gather.11.cloned.1.call-update) | async-done | bytes 4194320 | tf_op jit(solution)/shard_map/while/body/eval_jaxpr/all_gather | solution.py:57
  316.9 11.7 cholesky.1240
  339.3 11.7 cholesky.1243
  351.0 10.2 custom-call.138
  361.9 11.7 cholesky.1245
  384.0 11.8 cholesky.1246
  401.8 10.6 while.27
  412.4 40.2 %custom-call.141 = f32[4,128,128]{1,2,0:T(8,128)S(1)} custom-call(f32[4,128,128]{2,1,0:T(8,128)} %get-tuple-element.446), custom_call_target="InvertDiagBlocksLowerTriangular" | custom-call | tf_op jit(solution)/shard_map/while/body/eval_jaxpr/jit(_solve_triangular)/triangular_solve | solution.py:43
  506.9 48.6 %all-gather.11.cloned.1.call-done = f32[2048,512]{1,0:T(8,128)} async-done(((f32[128,512]{1,0:T(8,128)}), f32[2048,512]{1,0:T(8,128)}) %all-gather.11.cloned.1.call-update) | async-done | bytes 4194320 | tf_op jit(solution)/shard_map/while/body/eval_jaxpr/all_gather | solution.py:57
  559.2 11.7 cholesky.1240
  581.6 11.7 cholesky.1243
  593.3 10.2 custom-call.138
  604.2 11.7 cholesky.1245
  626.4 11.8 cholesky.1246
  644.2 10.6 while.27
  654.8 40.2 %custom-call.141 = f32[4,128,128]{1,2,0:T(8,128)S(1)} custom-call(f32[4,128,128]{2,1,0:T(8,128)} %get-tuple-element.446), custom_call_target="InvertDiagBlocksLowerTriangular" | custom-call | tf_op jit(solution)/shard_map/while/body/eval_jaxpr/jit(_solve_triangular)/triangular_solve | solution.py:43
  749.3 48.3 %all-gather.11.cloned.1.call-done = f32[2048,512]{1,0:T(8,128)} async-done(((f32[128,512]{1,0:T(8,128)}), f32[2048,512]{1,0:T(8,128)}) %all-gather.11.cloned.1.call-update) | async-done | bytes 4194320 | tf_op jit(solution)/shard_map/while/body/eval_jaxpr/all_gather | solution.py:57
  801.2 11.7 cholesky.1240
  823.6 11.7 cholesky.1243
  846.2 11.7 cholesky.1245
  868.4 11.8 cholesky.1246
  886.2 10.6 while.27
  896.8 40.2 %custom-call.141 = f32[4,128,128]{1,2,0:T(8,128)S(1)} custom-call(f32[4,128,128]{2,1,0:T(8,128)} %get-tuple-element.446), custom_call_target="InvertDiagBlocksLowerTriangular" | custom-call | tf_op jit(solution)/shard_map/while/body/eval_jaxpr/jit(_solve_triangular)/triangular_solve | solution.py:43
  993.7 70.6 %all-gather.5.cloned.1.call-done = f32[1024,2048]{1,0:T(8,128)} async-done(((f32[64,2048]{1,0:T(8,128)}), f32[1024,2048]{1,0:T(8,128)}) %all-gather.5.cloned.1.call-update) | async-done | bytes 8388624 | tf_op jit(solution)/shard_map/all_gather | solution.py:106
  1064.3 11.4 convolution_negate_fusion
  1083.5 26.0 %all-to-all-done = f32[8,64,1024]{2,1,0:T(8,128)S(1)} async-done(((f32[8,64,1024]{2,1,0:T(8,128)}), f32[8,64,1024]{2,1,0:T(8,128)S(1)}, u32[]{:S(2)}, u32[]{:S(2)}) %all-to-all-start) | async-done | bytes 2097184 | tf_op jit(solution)/shard_map/all_to_all | solution.py:34
  1110.7 49.2 %all-gather.7.cloned.1.call-done = f32[1024,1024]{1,0:T(8,128)} async-done(((f32[64,1024]{1,0:T(8,128)}), f32[1024,1024]{1,0:T(8,128)}) %all-gather.7.cloned.1.call-update) | async-done | bytes 4194320 | tf_op jit(solution)/shard_map/all_gather | solution.py:83
  1162.7 34.8 %reduce-scatter.2.cloned.1.call-done = f32[128,1024]{1,0:T(8,128)} async-done(((f32[1024,1024]{1,0:T(8,128)}), f32[128,1024]{1,0:T(8,128)}) %reduce-scatter.2.cloned.1.call-update) | async-done | bytes 524304 | tf_op jit(solution)/shard_map/reduce_scatter | solution.py:23
  1200.0 33.5 %all-gather.9.cloned.1.call-done = f32[1024,1024]{1,0:T(8,128)} async-done(((f32[128,1024]{1,0:T(8,128)}), f32[1024,1024]{1,0:T(8,128)}) %all-gather.9.cloned.1.call-update) | async-done | bytes 4194320 | tf_op jit(solution)/shard_map/all_gather | solution.py:24
  1261.5 11.7 cholesky.347
  1289.5 11.9 cholesky.368
  1315.2 11.7 cholesky.395
  1340.9 11.9 cholesky.593
  1366.7 11.7 cholesky.612
  1392.6 11.7 cholesky.628
  1417.7 11.7 cholesky.644
  1442.5 11.7 cholesky.658
  1471.2 22.5 %while.24 = (s32[]{:T(128)}, f32[1024,1024]{1,0:T(8,128)}, s32[8,2]{0,1:T(2,128)S(1)}, f32[8,128,128]{2,1,0:T(8,128)S(1)}, s32[]{:T(128)}) while((s32[]{:T(128)}, f32[1024,1024]{1,0:T(8,128)}, s32[8,2]{0,1:T(2,128)S(1)}, f32[8,128,128]{2,1,0:T(8,128)S(1)}, s32[]{:T(128)}) %tuple.152), condition=%wide.while_cond.1, body=%wide.while_body.1.sunk | while | flops 2 | bytes 131189 | solution.py:43
  1493.7 78.8 %custom-call.110 = f32[8,128,128]{1,2,0:T(8,128)S(1)} custom-call(f32[8,128,128]{2,1,0:T(8,128)S(1)} %get-tuple-element.178), custom_call_target="InvertDiagBlocksLowerTriangular" | custom-call | tf_op jit(solution)/shard_map/jit(_solve_triangular)/triangular_solve | solution.py:43
  (451 shorter events, 563.2 us)
Async XLA Ops:
  8.0 4.6 copy-start.7
  12.8 58.1 %all-gather.11.cloned.1.call-start = ((), (), s32[]{:S(2)}) async-start(), calls=%async_computation.6 | async-start | bytes 4456448 | tf_op jit(solution)/shard_map/while/body/eval_jaxpr/all_gather | solution.py:57
  170.1 46.8 %copy-start.1 = (f32[512,512]{1,0:T(8,128)}, f32[512,512]{1,0:T(8,128)S(1)}, u32[]{:S(2)}) copy-start(f32[512,512]{1,0:T(8,128)S(1)} %get-tuple-element.524) | copy-start | bytes 3145732 | tf_op jit(solution)/shard_map/while
  210.3 6.6 copy-start
  238.6 1.8 copy-start.2
  240.4 4.9 copy-start.3
  258.6 54.6 %all-gather.11.cloned.1.call-start = ((), (), s32[]{:S(2)}) async-start(), calls=%async_computation.6 | async-start | bytes 4456448 | tf_op jit(solution)/shard_map/while/body/eval_jaxpr/all_gather | solution.py:57
  412.4 46.8 %copy-start.1 = (f32[512,512]{1,0:T(8,128)}, f32[512,512]{1,0:T(8,128)S(1)}, u32[]{:S(2)}) copy-start(f32[512,512]{1,0:T(8,128)S(1)} %get-tuple-element.524) | copy-start | bytes 3145732 | tf_op jit(solution)/shard_map/while
  452.6 6.6 copy-start
  480.9 1.8 copy-start.2
  482.7 4.9 copy-start.3
  500.9 54.6 %all-gather.11.cloned.1.call-start = ((), (), s32[]{:S(2)}) async-start(), calls=%async_computation.6 | async-start | bytes 4456448 | tf_op jit(solution)/shard_map/while/body/eval_jaxpr/all_gather | solution.py:57
  654.8 46.8 %copy-start.1 = (f32[512,512]{1,0:T(8,128)}, f32[512,512]{1,0:T(8,128)S(1)}, u32[]{:S(2)}) copy-start(f32[512,512]{1,0:T(8,128)S(1)} %get-tuple-element.524) | copy-start | bytes 3145732 | tf_op jit(solution)/shard_map/while
  694.9 6.6 copy-start
  723.3 1.8 copy-start.2
  725.0 4.9 copy-start.3
  743.2 54.3 %all-gather.11.cloned.1.call-start = ((), (), s32[]{:S(2)}) async-start(), calls=%async_computation.6 | async-start | bytes 4456448 | tf_op jit(solution)/shard_map/while/body/eval_jaxpr/all_gather | solution.py:57
  896.8 46.8 %copy-start.1 = (f32[512,512]{1,0:T(8,128)}, f32[512,512]{1,0:T(8,128)S(1)}, u32[]{:S(2)}) copy-start(f32[512,512]{1,0:T(8,128)S(1)} %get-tuple-element.524) | copy-start | bytes 3145732 | tf_op jit(solution)/shard_map/while
  936.9 6.6 copy-start
  965.3 1.8 copy-start.2
  967.0 4.9 copy-start.3
  991.0 73.3 %all-gather.5.cloned.1.call-start = ((), (), s32[]{:S(2)}) async-start(), calls=%async_computation.2 | async-start | bytes 8912896 | tf_op jit(solution)/shard_map/all_gather | solution.py:106
  1075.7 7.7 copy-start.8
  1075.7 34.1 %copy-start.6 = (f32[64,1024]{1,0:T(8,128)S(1)}, f32[64,1024]{1,0:T(8,128)}, u32[]{:S(2)}) copy-start(f32[64,1024]{1,0:T(8,128)} %param.15) | copy-start | bytes 786436
  1078.1 31.4 %all-to-all-start = ((f32[8,64,1024]{2,1,0:T(8,128)}), f32[8,64,1024]{2,1,0:T(8,128)S(1)}, u32[]{:S(2)}, u32[]{:S(2)}) async-start(f32[8,64,1024]{2,1,0:T(8,128)} %bitcast.282), calls=%async_computation | async-start | bytes 4194304 | tf_op jit(solution)/shard_map/all_to_all | solution.py:34
  1083.3 76.6 %all-gather.7.cloned.1.call-start = ((), (), s32[]{:S(2)}) async-start(), calls=%async_computation.3 | async-start | bytes 4456448 | tf_op jit(solution)/shard_map/all_gather | solution.py:83
  1110.6 87.0 %reduce-scatter.2.cloned.1.call-start = ((), (), s32[]{:S(2)}) async-start(), calls=%async_computation.4 | async-start | bytes 4718592 | tf_op jit(solution)/shard_map/reduce_scatter | solution.py:23
  1162.6 70.8 %all-gather.9.cloned.1.call-start = ((), (), s32[]{:S(2)}) async-start(), calls=%async_computation.5 | async-start | bytes 4718592 | tf_op jit(solution)/shard_map/all_gather | solution.py:24
  1259.6 1.9 copy-start.4
  1464.6 107.9 %copy-start.5 = (f32[64,1024]{1,0:T(8,128)S(1)}, f32[64,1024]{1,0:T(8,128)}, u32[]{:S(2)}) copy-start(f32[64,1024]{1,0:T(8,128)} %fusion.101) | copy-start | bytes 786436
Sparse Core Ops, SparseCore 0:
  16.3 54.5 all-gather.10
  262.1 51.0 all-gather.10
  504.4 51.0 all-gather.10
  746.4 51.0 all-gather.10
Sparse Core Ops, SparseCore 1:
  993.8 70.4 all-gather.4
  1110.7 49.1 all-gather.6
  1162.7 34.8 reduce-scatter.1
  1199.3 34.1 all-gather.8
where the time goes:
time: 1600 us; the launch traced here: 1590 us
  other arithmetic  781 us (49%)
  waiting for transfers between devices  412 us (26%)
  matrix products  208 us (13%)
  local copies, waits for them, and re-layouts  131 us (8%)
  loops' own time  33.8 us (2%)
  between operations  21.1 us (1%)
    another operation x56, other arithmetic, advance(): factor = jnp.linalg.cholesky(mirror_lower(diag_block))  316 us
    another operation x15, other arithmetic, solve_right(): jax.scipy.linalg.solve_triangular(lower_factor, matrix.T, lower=True)  251 us
    all_gather x4, waiting for transfers between devices, advance(): gathered = lax.all_gather(column, 'front', axis=0, tiled=True)  197 us
    another operation x30, other arithmetic, parent_whole(): factor = jnp.linalg.cholesky(mirror_lower(pivot_block))  172 us
    another operation x71, matrix products, solve_right(): jax.scipy.linalg.solve_triangular(lower_factor, matrix.T, lower=True)  113 us
    all_gather x1, waiting for transfers between devices, on_device(): lax.all_gather(landing_piece, 'front', axis=0, tiled=True)  70.6 us
    another operation x72, local copies, waits for them, and re-layouts  64.7 us
    all_gather x1, waiting for transfers between devices, parent_whole(): group_rows = lax.all_gather(assembled, 'front', axis=0, tiled=True)  49.2 us
  transfers between devices with their start and end apart: 9, of which 9 were waited for; matrix products, arithmetic and copies ran while one was open for 1% of the time, Pallas kernels for 0%

commit v1 on v0

v1 whole, which is shorter than its diff:
```python
import functools

import jax
import jax.numpy as jnp
from jax import lax
from jax.experimental import pallas as pl
from jax.experimental.pallas import tpu as pltpu
from jax.sharding import PartitionSpec as P

BLOCK = 128
F32, BF = jnp.float32, jnp.bfloat16
NT = (((1,), (1,)), ((), ()))
HIGHEST_PRECISION = lax.Precision.HIGHEST


def factor_block(load_row, store_u, store_e, n=128, sb=8):
    nb = n // sb
    W = [load_row(v) for v in range(nb)]
    lane = lax.broadcasted_iota(jnp.int32, (sb, n), 1)
    sub = lax.broadcasted_iota(jnp.int32, (sb, n), 0)
    for b in range(nb):
        base = b * sb
        inblk = (lane >= base) & (lane < base + sb)
        R = W[b]
        S = [jnp.broadcast_to(R[:, base + j:base + j + 1], (sb, n)) for j in range(sb)]
        F = {}
        for j in range(sb):
            for i in range(j, sb):
                F[i, j] = jnp.broadcast_to(S[j][i:i + 1, :], (sb, n))
        rinv = []
        for j in range(sb):
            r = lax.rsqrt(F[j, j])
            rinv.append(r)
            for i in range(j, sb):
                F[i, j] = F[i, j] * r
            for c in range(j + 1, sb):
                for i in range(c, sb):
                    F[i, c] = F[i, c] - F[i, j] * F[c, j]
        RI = jnp.where(inblk, (lane - base == sub).astype(jnp.float32), R)
        u = []
        for j in range(sb):
            t = jnp.broadcast_to(RI[j:j + 1, :], (sb, n))
            for m in range(j):
                t = t - F[j, m] * u[m]
            u.append(t * rinv[j])
        e = u[0]
        for j in range(1, sb):
            e = jnp.where(sub == j, u[j], e)
        store_e(b, jnp.where(lane < base + sb, e, 0.0))
        d = jnp.zeros((sb, n), jnp.float32)
        for j in range(sb):
            for c in range(j, sb):
                d = jnp.where((sub == j) & (lane == base + c), F[c, j], d)
        store_u(b, jnp.where(inblk, d, jnp.where(lane < base, 0.0, e)))
        for v in range(b + 1, nb):
            C = []
            acc = jnp.where(inblk, 0.0, W[v])
            for j in range(sb):
                c = jnp.broadcast_to(W[v][:, base + j:base + j + 1], (sb, n))
                for m in range(j):
                    c = c - C[m] * F[j, m]
                c = c * rinv[j]
                C.append(c)
                acc = acc - c * u[j]
            W[v] = acc


def split(x):
    hi = x.astype(BF)
    return hi, (x - hi.astype(F32)).astype(BF)

def dot3(ah, al, bh, bl):
    d = functools.partial(lax.dot_general, dimension_numbers=NT, preferred_element_type=F32)
    return d(ah, bh) + (d(ah, bl) + d(al, bh))

def chol_kernel(n, m, a_ref, c_ref, l_out, c_out, T, Lh, Ll, U, E, Eh, El, *, own, row0):
    full = n // 256
    row_ids = None

    def chunks(lo, body):
        def step(r, _):
            body(pl.multiple_of(r * 256, 256), 256)
            return 0
        lax.fori_loop(lo, full, step, 0)
        body(n, m)

    def stage(p, _):
        k, half = p // 2, p % 2
        for kk in range(full):
            @pl.when(p == 2 * kk)
            def _():
                def upd(r, cnt):
                    rows = pl.ds(r, cnt)
                    if isinstance(r, int) and r >= n:
                        x = c_ref[:, 256 * kk:256 * kk + 256]
                    else:
                        x = a_ref[rows, 256 * kk:256 * kk + 256]
                    if kk:
                        kr = pl.ds(256 * kk, 256)
                        x = x - dot3(Lh[rows, :256 * kk], Ll[rows, :256 * kk], Lh[kr, :256 * kk], Ll[kr, :256 * kk])
                    T[rows, :] = x
                chunks(kk, upd)
        prow = pl.multiple_of(p * 128, 128)
        pcol = pl.ds(prow, 128)
        hcol = pl.ds(pl.multiple_of(half * 128, 128), 128)

        @pl.when(half == 1)
        def _():
            qcol = pl.ds(pl.multiple_of(prow - 128, 128), 128)
            bh, bl = Lh[pcol, qcol], Ll[pcol, qcol]
            def upd(r, cnt):
                rows = pl.ds(r, cnt)
                T[rows, 128:256] = T[rows, 128:256] - dot3(Lh[rows, qcol], Ll[rows, qcol], bh, bl)
            upd(prow, 128)
            chunks(k + 1, upd)

        def su(b, x): U[pl.ds(8 * b, 8), :] = x
        def se(b, x): E[pl.ds(8 * b, 8), :] = x
        factor_block(lambda v: T[pl.ds(pl.multiple_of(prow + 8 * v, 8), 8), hcol], su, se)
        eh, el = split(E[...])
        Eh[...] = eh
        El[...] = el

        def solve(r, cnt):
            rows = pl.ds(r, cnt)
            th, tl = split(T[rows, hcol])
            x = dot3(th, tl, Eh[...], El[...])
            T[rows, hcol] = x
            xh, xl = split(x)
            Lh[rows, pcol] = xh
            Ll[rows, pcol] = xl

        @pl.when(half == 0)
        def _():
            solve(pl.multiple_of(prow + 128, 128), 128)
        chunks(k + 1, solve)
        T[pl.ds(prow, 128), hcol] = U[...].T
        c_out[:, pcol] = T[n:n + m, hcol]
        mine = T[pl.ds(pl.multiple_of(row0, own), own), hcol]
        l_out[:, pcol] = jnp.where(prow < row0 + own, mine, 0.0)
        return 0

    lax.fori_loop(0, n // 128, stage, 0)

def chol_call(n, m, own, get_row0, vmem=60 << 20):
    def kern(*refs):
        chol_kernel(n, m, *refs, own=own, row0=get_row0())
    return pl.pallas_call(
        kern,
        out_shape=[jax.ShapeDtypeStruct((own, n), F32), jax.ShapeDtypeStruct((m, n), F32)],
        in_specs=[pl.BlockSpec(memory_space=pltpu.VMEM)] * 2,
        out_specs=[pl.BlockSpec(memory_space=pltpu.VMEM)] * 2,
        scratch_shapes=[pltpu.VMEM((n + m, 256), F32), pltpu.VMEM((n + m, n), BF), pltpu.VMEM((n + m, n), BF),
                        pltpu.VMEM((128, 128), F32), pltpu.VMEM((128, 128), F32),
                        pltpu.VMEM((128, 128), BF), pltpu.VMEM((128, 128), BF)],
        compiler_params=pltpu.CompilerParams(vmem_limit_bytes=vmem),
    )


def sent_and_summed(array, axis):
    pieces = array.reshape(lax.axis_size(axis), -1, array.shape[1])
    arrived = lax.all_to_all(pieces, axis, split_axis=0, concat_axis=0, tiled=True)
    return arrived.sum(axis=0)


def on_device(child_pivot, child_coupling, parent_arrow, row_map, block_pattern):
    own_rows = child_pivot[0]
    parent_index = row_map[0]
    row_count, pivot_count = own_rows.shape
    parent_count, pivots = parent_arrow.shape
    front_index = lax.axis_index("front")
    front_groups = lax.axis_size("front")
    child_whole = lax.all_gather(own_rows, "front", axis=0, tiled=True)
    lower_rows, coupling = chol_call(
        pivot_count, row_count, row_count, lambda: lax.axis_index("front") * row_count
    )(child_whole, child_coupling[0])
    slot_index = (
        parent_index // parent_count // front_groups * parent_count + parent_index % parent_count
    )
    spread_rows = lax.axis_size("bulk") * parent_count
    routing = (slot_index[:, None] == jnp.arange(spread_rows)[None, :]).astype(F32)
    landing_piece = jnp.dot(routing[:, :parent_count].T, coupling, precision=HIGHEST_PRECISION)
    landing = lax.all_gather(landing_piece, "front", axis=0, tiled=True)
    reached = -jnp.dot(coupling, landing.T, precision=lax.Precision.HIGH)
    routed = jnp.dot(routing.T, reached, precision=HIGHEST_PRECISION)
    device_index = lax.axis_index("bulk") * front_groups + front_index
    first_row = device_index * parent_count
    block_rows = (first_row + jnp.arange(parent_count)) // BLOCK
    picker = (block_rows[:, None] == jnp.arange(block_pattern.shape[0])[None, :]).astype(F32)
    row_mask = jnp.dot(picker, block_pattern.astype(F32), precision=HIGHEST_PRECISION)
    masked = parent_arrow * jnp.repeat(row_mask, BLOCK, axis=1)
    top = routed[:parent_count] + jnp.where(lax.axis_index("bulk") == 0, masked, 0.0)
    top = lax.psum(top, "bulk")
    pivot_block = lax.all_gather(top, "front", axis=0, tiled=True)
    assembled = masked + sent_and_summed(routed, "bulk")
    factor_rows, solved = chol_call(
        pivots, parent_count, parent_count, lambda: lax.axis_index("front") * parent_count
    )(pivot_block, assembled)
    parent_rows = jnp.where(first_row < pivots, factor_rows, solved)
    return (lower_rows[None], coupling[None], parent_rows)


def solution(mesh):
    placed = (
        P("bulk", "front", None),
        P("bulk", "front", None),
        P(("bulk", "front"), None),
        P("bulk", "front"),
        P(),
    )
    return jax.shard_map(
        on_device,
        mesh=mesh,
        in_specs=placed,
        out_specs=(P("bulk", "front", None), P("bulk", "front", None), P(("bulk", "front"), None)),
        check_vma=False,
    )
```

time: 1600 us -> 525 us (0.33)
  other arithmetic: 781 us -> 4.47 us
  matrix products: 208 us -> 13.2 us
  Pallas kernels: 0 us -> 163 us
  local copies, waits for them, and re-layouts: 131 us -> 0.13 us
  waiting for transfers between devices: 412 us -> 324 us
  loops' own time: 33.8 us -> 0 us
    another operation x101 -> x0, other arithmetic: 739 us -> none  [the longest x56 316 us: advance(): factor = jnp.linalg.cholesky(mirror_lower(diag_block))]
    pallas_call x0 -> x2, Pallas kernels: none -> 163 us  [the longest x1 117 us: on_device(): chol_call(pivot_count, row_count, row_count, lambda: lax.axis_index('fron...]
    another operation x109 -> x0, matrix products: 144 us -> none  [the longest x71 113 us: solve_right(): jax.scipy.linalg.solve_triangular(lower_factor, matrix.T, lower=True)]
    all_gather x7 -> x3, waiting for transfers between devices: 351 us -> 241 us  [the longest x1 116 us: on_device(): child_whole = lax.all_gather(own_rows, 'front', axis=0, tiled=True)]
    another operation x101 -> x0, local copies, waits for them, and re-layouts: 67.8 us -> none
    psum x0 -> x1, waiting for transfers between devices: none -> 56.3 us  [on_device(): top = lax.psum(top, 'bulk')]
    dot_general x12 -> x4, matrix products: 64.3 us -> 13.2 us  [the longest x1 7.96 us: on_device(): reached = -jnp.dot(coupling, landing.T, precision=lax.Precision.HIGH)]
    reduce_scatter x1 -> x0, waiting for transfers between devices: 34.8 us -> none  [from_root(): own = lax.psum_scatter(padded, axis, scatter_dimension=0, tiled=True)]
  transfers between devices with their start and end apart: 9 -> 5, of which waited for: 9 -> 5; matrix products, arithmetic and copies ran while one was open for 1% -> 0% of each run, Pallas kernels for 0% -> 0%
where the time goes in v1:
time: 525 us; the launch traced here: 524 us
  waiting for transfers between devices  324 us (62%)
  Pallas kernels  163 us (31%)
  between operations  13.8 us (3%)
  matrix products  13.2 us (3%)
  starting transfers between devices  5.25 us (1%)
    pallas_call x1, Pallas kernels, on_device(): chol_call(pivot_count, row_count, row_count, lambda: lax.axis_index('fron...  117 us
    all_gather x1, waiting for transfers between devices, on_device(): child_whole = lax.all_gather(own_rows, 'front', axis=0, tiled=True)  116 us
    all_gather x1, waiting for transfers between devices, on_device(): landing = lax.all_gather(landing_piece, 'front', axis=0, tiled=True)  70.6 us
    psum x1, waiting for transfers between devices, on_device(): top = lax.psum(top, 'bulk')  56.3 us
    all_gather x1, waiting for transfers between devices, on_device(): pivot_block = lax.all_gather(top, 'front', axis=0, tiled=True)  54.5 us
    pallas_call x1, Pallas kernels, on_device(): chol_call(pivots, parent_count, parent_count, lambda: lax.axis_index('fro...  46 us
    all_to_all x1, waiting for transfers between devices, sent_and_summed(): lax.all_to_all(pieces, axis, split_axis=0, concat_axis=0, tiled=True)  26 us
  transfers between devices with their start and end apart: 5, of which 5 were waited for; matrix products, arithmetic and copies ran while one was open for 0% of the time, Pallas kernels for 0%

profile of v1, /device:TPU:1, one launch (start us, length us, event | category | flops | bytes accessed | tf_op | source)
XLA Modules:
  0.0 524.3 jit_solution(562486347146470613)
XLA Ops:
  7.2 0.0 all-gather.9.cloned.1.call-start
  7.2 0.7 all-gather.9.cloned.1.call-update
  7.9 0.0 all-gather.5.cloned.1.call-start
  7.9 0.7 fusion.7
  8.6 0.1 iota_compare_fusion
  8.7 115.8 %all-gather.9.cloned.1.call-done = f32[1,2048,2048]{2,1,0:T(8,128)} async-done(((f32[1,128,2048]{2,1,0:T(8,128)}), f32[1,2048,2048]{2,1,0:T(8,128)}) %all-gather.9.cloned.1.call-update) | async-done | bytes 16777232 | tf_op jit(solution)/shard_map/all_gather | solution.py:173
  124.5 117.5 %shard_map.76 = (f32[128,2048]{1,0:T(8,128)}, f32[128,2048]{1,0:T(8,128)}) custom-call(f32[2048,2048]{1,0:T(8,128)} %bitcast.29, f32[128,2048]{1,0:T(8,128)} %bitcast.31), custom_call_target="tpu_custom_call" | custom-call | tf_op jit(solution)/shard_map/pallas_call | solution.py:174
  242.0 2.6 fusion.1
  244.6 0.0 all-gather.5.cloned.1.call-update
  244.6 0.0 copy-start.1
  244.6 0.0 copy-start
  244.6 70.6 %all-gather.5.cloned.1.call-done = f32[1024,2048]{1,0:T(8,128)} async-done(((f32[64,2048]{1,0:T(8,128)}), f32[1024,2048]{1,0:T(8,128)}) %all-gather.5.cloned.1.call-update) | async-done | bytes 8388624 | tf_op jit(solution)/shard_map/all_gather | solution.py:183
  315.3 8.0 %convolution_negate_fusion = f32[128,1024]{1,0:T(8,128)S(1)} fusion(f32[128,2048]{1,0:T(8,128)} %get-tuple-element.8, f32[1024,2048]{1,0:T(8,128)} %all-gather.5.cloned.1.call-done), kind=kOutput, calls=%fused_computation | convolution fusion | flops 1610743808 | bytes 9961472 | tf_op jit(solution)/shard_map/dot_general | solution.py:184
  323.2 2.4 fusion.5
  325.6 5.1 all-to-all-start
  330.8 0.0 all-reduce.2.cloned.1.call-start
  330.8 0.0 copy-done.1
  330.8 0.2 fusion.3
  331.0 26.0 %all-to-all-done = f32[8,64,1024]{2,1,0:T(8,128)S(1)} async-done(((f32[8,64,1024]{2,1,0:T(8,128)}), f32[8,64,1024]{2,1,0:T(8,128)S(1)}, u32[]{:S(2)}, u32[]{:S(2)}) %all-to-all-start) | async-done | bytes 2097184 | tf_op jit(solution)/shard_map/all_to_all | solution.py:162
  357.0 0.1 reduce_sum.9
  357.1 0.1 broadcast_in_dim.19
  357.2 0.0 copy-done
  357.3 1.9 fusion
  359.1 0.0 all-reduce.2.cloned.1.call-update
  359.1 0.0 all-gather.7.cloned.1.call-start
  359.2 56.3 %all-reduce.2.cloned.1.call-done = f32[64,1024]{1,0:T(8,128)} async-done(((f32[64,1024]{1,0:T(8,128)}), f32[64,1024]{1,0:T(8,128)}) %all-reduce.2.cloned.1.call-update) | async-done | bytes 262160 | tf_op jit(solution)/shard_map/psum | solution.py:193
  415.5 0.0 all-gather.7.cloned.1.call-update
  415.6 54.5 %all-gather.7.cloned.1.call-done.refs_0_ = f32[1024,1024]{1,0:T(8,128)} async-done(((f32[64,1024]{1,0:T(8,128)}), f32[1024,1024]{1,0:T(8,128)}) %all-gather.7.cloned.1.call-update) | async-done | bytes 4194320 | tf_op jit(solution)/shard_map/all_gather | solution.py:194
  470.1 46.0 %shard_map.77 = (f32[64,1024]{1,0:T(8,128)}, f32[64,1024]{1,0:T(8,128)}) custom-call(f32[1024,1024]{1,0:T(8,128)} %all-gather.7.cloned.1.call-done.refs_0_, f32[64,1024]{1,0:T(8,128)} %get-tuple-element.11.refs_1_), custom_call_target="tpu_custom_call" | custom-call | tf_op jit(solution)/shard_map/pallas_call | solution.py:196
  516.1 1.7 broadcast_select_fusion
  (1 shorter events, 0.0 us)
Async XLA Ops:
  7.2 117.4 %all-gather.9.cloned.1.call-start = ((), (), s32[]{:S(2)}) async-start(), calls=%async_computation.4 | async-start | bytes 17825792 | tf_op jit(solution)/shard_map/all_gather | solution.py:173
  7.9 307.4 %all-gather.5.cloned.1.call-start = ((), (), s32[]{:S(2)}) async-start(), calls=%async_computation.1 | async-start | bytes 8912896 | tf_op jit(solution)/shard_map/all_gather | solution.py:183
  244.6 86.2 %copy-start.1 = (s32[64,8]{0,1:T(8,128)S(1)}, s32[64,8]{0,1:T(8,128)}, u32[]{:S(2)}) copy-start(s32[64,8]{0,1:T(8,128)} %param.9) | copy-start | bytes 6148
  244.6 112.6 %copy-start = (f32[64,1024]{1,0:T(8,128)S(1)}, f32[64,1024]{1,0:T(8,128)}, u32[]{:S(2)}) copy-start(f32[64,1024]{1,0:T(8,128)} %param.7) | copy-start | bytes 786436
  325.6 31.3 %all-to-all-start = ((f32[8,64,1024]{2,1,0:T(8,128)}), f32[8,64,1024]{2,1,0:T(8,128)S(1)}, u32[]{:S(2)}, u32[]{:S(2)}) async-start(f32[8,64,1024]{2,1,0:T(8,128)} %bitcast.5), calls=%async_computation | async-start | bytes 4194304 | tf_op jit(solution)/shard_map/all_to_all | solution.py:162
  330.8 84.8 %all-reduce.2.cloned.1.call-start = ((), (), s32[]{:S(2)}) async-start(), calls=%async_computation.2 | async-start | bytes 524288 | tf_op jit(solution)/shard_map/psum | solution.py:193
  359.1 111.0 %all-gather.7.cloned.1.call-start = ((), (), s32[]{:S(2)}) async-start(), calls=%async_computation.3 | async-start | bytes 4456448 | tf_op jit(solution)/shard_map/all_gather | solution.py:194
Sparse Core Ops, SparseCore 0:
  10.1 114.3 all-gather.8
  244.7 70.4 all-gather.4
  359.3 56.2 all-reduce.1
  417.5 52.5 all-gather.6

commit v2 on v1

v2 whole, which is shorter than its diff:
```python
import functools

import jax
import jax.numpy as jnp
from jax import lax
from jax.experimental import pallas as pl
from jax.experimental.pallas import tpu as pltpu
from jax.sharding import PartitionSpec as P

BLOCK = 128
F32, BF = jnp.float32, jnp.bfloat16
NT = (((1,), (1,)), ((), ()))
MESH = pl.DeviceIdType.MESH
HIGHEST_PRECISION = lax.Precision.HIGHEST


def factor_block(load_row, store_u, store_e, n=128, sb=8):
    nb = n // sb
    W = [load_row(v) for v in range(nb)]
    lane = lax.broadcasted_iota(jnp.int32, (sb, n), 1)
    sub = lax.broadcasted_iota(jnp.int32, (sb, n), 0)
    for b in range(nb):
        base = b * sb
        inblk = (lane >= base) & (lane < base + sb)
        R = W[b]
        S = [jnp.broadcast_to(R[:, base + j:base + j + 1], (sb, n)) for j in range(sb)]
        F = {}
        for j in range(sb):
            for i in range(j, sb):
                F[i, j] = jnp.broadcast_to(S[j][i:i + 1, :], (sb, n))
        rinv = []
        for j in range(sb):
            r = lax.rsqrt(F[j, j])
            rinv.append(r)
            for i in range(j, sb):
                F[i, j] = F[i, j] * r
            for c in range(j + 1, sb):
                for i in range(c, sb):
                    F[i, c] = F[i, c] - F[i, j] * F[c, j]
        RI = jnp.where(inblk, (lane - base == sub).astype(jnp.float32), R)
        u = []
        for j in range(sb):
            t = jnp.broadcast_to(RI[j:j + 1, :], (sb, n))
            for m in range(j):
                t = t - F[j, m] * u[m]
            u.append(t * rinv[j])
        e = u[0]
        for j in range(1, sb):
            e = jnp.where(sub == j, u[j], e)
        store_e(b, jnp.where(lane < base + sb, e, 0.0))
        d = jnp.zeros((sb, n), jnp.float32)
        for j in range(sb):
            for c in range(j, sb):
                d = jnp.where((sub == j) & (lane == base + c), F[c, j], d)
        store_u(b, jnp.where(inblk, d, jnp.where(lane < base, 0.0, e)))
        for v in range(b + 1, nb):
            C = []
            acc = jnp.where(inblk, 0.0, W[v])
            for j in range(sb):
                c = jnp.broadcast_to(W[v][:, base + j:base + j + 1], (sb, n))
                for m in range(j):
                    c = c - C[m] * F[j, m]
                c = c * rinv[j]
                C.append(c)
                acc = acc - c * u[j]
            W[v] = acc


def split(x):
    hi = x.astype(BF)
    return hi, (x - hi.astype(F32)).astype(BF)

def dot3(ah, al, bh, bl):
    d = functools.partial(lax.dot_general, dimension_numbers=NT, preferred_element_type=F32)
    return d(ah, bh) + (d(ah, bl) + d(al, bh))


def dynamic(p, size):
    return pl.ds(pl.multiple_of(p * size, size), size)


def chol_stage(p, n, m, block, extra, T, Lh, Ll, U, E, Eh, El, *, before, after_factor, before_rest):
    full = n // 256
    k, half = p // 2, p % 2
    prow = pl.multiple_of(p * 128, 128)
    pcol = pl.ds(prow, 128)
    qcol = pl.ds(pl.multiple_of(prow - half * 128, 128), 128)
    hcol = dynamic(half, 128)

    def update(kk, r, cnt):
        rows = pl.ds(r, cnt)
        x = extra(kk) if isinstance(r, int) and r >= n else block(kk, rows)
        if kk:
            kr = pl.ds(256 * kk, 256)
            x = x - dot3(Lh[rows, :256 * kk], Ll[rows, :256 * kk], Lh[kr, :256 * kk], Ll[kr, :256 * kk])
        T[rows, :] = x

    def half_update(r, cnt):
        rows = pl.ds(r, cnt)
        T[rows, 128:256] = T[rows, 128:256] - dot3(Lh[rows, qcol], Ll[rows, qcol], Lh[pcol, qcol], Ll[pcol, qcol])

    def solve(r, cnt):
        rows = pl.ds(r, cnt)
        th, tl = split(T[rows, hcol])
        x = dot3(th, tl, Eh[...], El[...])
        T[rows, hcol] = x
        xh, xl = split(x)
        Lh[rows, pcol] = xh
        Ll[rows, pcol] = xl

    def rest(body):
        def step(r, _):
            body(pl.multiple_of(r * 256, 256), 256)
            return 0
        lax.fori_loop(k + 1, full, step, 0)
        body(n, m)

    before(p)
    for kk in range(full):
        @pl.when(p == 2 * kk)
        def _():
            update(kk, 256 * kk, 256)

    @pl.when(half == 1)
    def _():
        half_update(prow, 128)

    def su(b, x): U[pl.ds(8 * b, 8), :] = x
    def se(b, x): E[pl.ds(8 * b, 8), :] = x
    factor_block(lambda v: T[pl.ds(pl.multiple_of(prow + 8 * v, 8), 8), hcol], su, se)
    eh, el = split(E[...])
    Eh[...] = eh
    El[...] = el
    after_factor(p)

    @pl.when(half == 0)
    def _():
        solve(pl.multiple_of(prow + 128, 128), 128)
    before_rest(p)
    for kk in range(full):
        @pl.when(p == 2 * kk)
        def _():
            def both(r, cnt):
                update(kk, r, cnt)
                solve(r, cnt)
            rest(both)

    @pl.when(half == 1)
    def _():
        def both(r, cnt):
            half_update(r, cnt)
            solve(r, cnt)
        rest(both)
    T[pl.ds(prow, 128), hcol] = U[...].T


def put_rows(p, n, m, own, row0, T, l_out, c_out):
    hcol, pcol = dynamic(p % 2, 128), dynamic(p, 128)
    c_out[:, pcol] = T[n:n + m, hcol]
    mine = T[pl.ds(pl.multiple_of(row0, own), own), hcol]
    l_out[:, pcol] = jnp.where(p * 128 < row0 + own, mine, 0.0)


def chol_scratch(n, m):
    return [pltpu.VMEM((n + m, 256), F32), pltpu.VMEM((n + m, n), BF), pltpu.VMEM((n + m, n), BF),
            pltpu.VMEM((128, 128), F32), pltpu.VMEM((128, 128), F32),
            pltpu.VMEM((128, 128), BF), pltpu.VMEM((128, 128), BF)]


def nothing(p):
    pass


def parent_kernel(n, m, a_ref, c_ref, l_out, c_out, *scratch):
    T = scratch[0]
    row0 = lax.axis_index("front") * m

    def stage(p, _):
        chol_stage(
            p, n, m,
            lambda kk, rows: a_ref[rows, 256 * kk:256 * kk + 256],
            lambda kk: c_ref[:, 256 * kk:256 * kk + 256],
            *scratch, before=nothing, after_factor=nothing, before_rest=nothing,
        )
        put_rows(p, n, m, m, row0, T, l_out, c_out)
        return 0
    lax.fori_loop(0, n // 128, stage, 0)


def parent_call(n, m):
    return pl.pallas_call(
        functools.partial(parent_kernel, n, m),
        out_shape=[jax.ShapeDtypeStruct((m, n), F32)] * 2,
        in_specs=[pl.BlockSpec(memory_space=pltpu.VMEM)] * 2,
        out_specs=[pl.BlockSpec(memory_space=pltpu.VMEM)] * 2,
        scratch_shapes=chol_scratch(n, m),
        compiler_params=pltpu.CompilerParams(vmem_limit_bytes=40 << 20),
    )


def child_kernel(n, m, land, groups, side, a_ref, c_ref, hit_ref, l_out, c_out, reach,
                 G, LG, own_sem, arrive, first_send, relay_send, land_arrive, land_first, land_relay, *scratch):
    T, Lh, Ll = scratch[0], scratch[1], scratch[2]
    stages, rows_own = n // 128, n // groups
    me = lax.axis_index("front")
    mx, mz = me // side, me % side
    own_parity = (mx + mz) % 2

    def along_z(d):
        return mx * side + (mz + d) % side

    def along_x(d):
        return (mx + d) % side * side + mz

    barrier = pltpu.get_barrier_semaphore()
    for d in range(1, groups):
        pl.semaphore_signal(barrier, inc=1, device_id={"front": (me + d) % groups}, device_id_type=MESH)
    pl.semaphore_wait(barrier, groups - 1)

    def relayed(j):
        if j < side // 2:
            return mx * side + mx % 2 + 2 * j
        return ((mz + 1) % 2 + 2 * (j - side // 2)) * side + mz

    def is_relayed(f):
        even = (f // side + f % side) % 2 == 0
        return ((f // side == mx) & even) | ((f % side == mz) & jnp.logical_not(even))

    def send(src, dst, send_sem, recv_sem, to):
        return pltpu.make_async_remote_copy(src_ref=src, dst_ref=dst, send_sem=send_sem, recv_sem=recv_sem,
                                            device_id={"front": to}, device_id_type=MESH)

    def G_at(k, f):
        return G.at[k, dynamic(f, rows_own), :]

    def own_copy(k):
        return pltpu.make_async_copy(a_ref.at[:, dynamic(k, 256)], G_at(k, me), own_sem.at[k])

    def first(k, d):
        to = jnp.where(own_parity == 0, along_z(d), along_x(d))
        return send(a_ref.at[:, dynamic(k, 256)], G_at(k, me), first_send.at[k, d - 1], arrive.at[k, me], to)

    def relay(k, j, d):
        f = relayed(j)
        to = along_x(d) if j < side // 2 else along_z(d)
        return send(G_at(k, f), G_at(k, f), relay_send.at[k, j, d - 1], arrive.at[k, f], to)

    def arrival(k, f):
        return pltpu.make_async_copy(G_at(k, f), G_at(k, f), arrive.at[k, f])

    def has(k, f):
        return f // 2 >= k

    def start_first(k):
        @pl.when(has(k, me))
        def _():
            for d in range(1, side):
                first(k, d).start()
            own_copy(k).start()

    def start_relay(k):
        for j in range(side):
            f = relayed(j)

            @pl.when(has(k, f))
            def _():
                @pl.when(f != me)
                def _():
                    arrival(k, f).wait()

                @pl.when(f == me)
                def _():
                    own_copy(k).wait()
                for d in range(1, side):
                    relay(k, j, d).start()

    def wait_block(k, f):
        @pl.when((f != me) & jnp.logical_not(is_relayed(f)))
        def _():
            arrival(k, f).wait()

    def wait_blocks(k, lo, hi):
        def step(f, _):
            wait_block(k, f)
            return 0
        lax.fori_loop(lo, hi, step, 0)

    def LG_at(p, f):
        return LG.at[p, dynamic(f, land), :]

    def land_one(p, d):
        to = jnp.where(own_parity == 0, along_z(d), along_x(d))
        return send(LG_at(p, me), LG_at(p, me), land_first.at[d - 1], land_arrive.at[p, me], to)

    def land_two(p, j, d):
        f = relayed(j)
        to = along_x(d) if j < side // 2 else along_z(d)
        return send(LG_at(p, f), LG_at(p, f), land_relay.at[j, d - 1], land_arrive.at[p, f], to)

    def landed(p, f):
        return pltpu.make_async_copy(LG_at(p, f), LG_at(p, f), land_arrive.at[p, f])

    def land_start(p):
        for d in range(1, side):
            @pl.when(p > 0)
            def _():
                land_one(p - 1, d).wait_send()
            land_one(p, d).start()

    def land_pass(p):
        for j in range(side):
            f = relayed(j)

            @pl.when(f != me)
            def _():
                landed(p, f).wait()
            for d in range(1, side):
                @pl.when(p > 0)
                def _():
                    land_two(p - 1, j, d).wait_send()
                land_two(p, j, d).start()

    def land_use(p):
        def step(f, _):
            @pl.when((f != me) & jnp.logical_not(is_relayed(f)))
            def _():
                landed(p, f).wait()
            return 0
        lax.fori_loop(0, groups, step, 0)
        pcol = dynamic(p, 128)
        gh, gl = split(LG[p])
        reach[...] = reach[...] - dot3(Lh[n:n + m, pcol], Ll[n:n + m, pcol], gh, gl)

    for k in range(3):
        start_first(k)
    start_relay(0)
    for k in range(3, n // 256):
        start_first(k)
    start_relay(1)
    reach[...] = jnp.zeros_like(reach)

    def before(p):
        k = p // 2

        @pl.when(p % 2 == 0)
        def _():
            @pl.when(k + 2 < n // 256)
            def _():
                start_relay(k + 2)
            wait_blocks(k, 2 * k, 2 * k + 2)

    def after_factor(p):
        @pl.when(p > 0)
        def _():
            land_pass(p - 1)

    def before_rest(p):
        @pl.when(p % 2 == 0)
        def _():
            wait_blocks(p // 2, p // 2 * 2 + 2, groups)

    def stage(p, _):
        chol_stage(
            p, n, m,
            lambda kk, rows: G[kk, rows, :],
            lambda kk: c_ref[:, 256 * kk:256 * kk + 256],
            *scratch, before=before, after_factor=after_factor, before_rest=before_rest,
        )
        pcol = dynamic(p, 128)
        nn = functools.partial(jnp.dot, preferred_element_type=F32)
        LG[p, dynamic(me, land), :] = nn(hit_ref[...], Lh[n:n + m, pcol]) + nn(hit_ref[...], Ll[n:n + m, pcol])
        put_rows(p, n, m, rows_own, me * rows_own, T, l_out, c_out)

        @pl.when(p >= 3)
        def _():
            land_use(p - 3)
        land_start(p)
        return 0
    lax.fori_loop(0, stages, stage, 0)
    land_use(stages - 3)
    land_pass(stages - 1)
    land_use(stages - 2)
    land_use(stages - 1)
    for d in range(1, side):
        land_one(stages - 1, d).wait_send()
        for j in range(side):
            land_two(stages - 1, j, d).wait_send()

    def drain(k, _):
        @pl.when(has(k, me))
        def _():
            for d in range(1, side):
                first(k, d).wait_send()
        for j in range(side):
            @pl.when(has(k, relayed(j)))
            def _():
                for d in range(1, side):
                    relay(k, j, d).wait_send()
        return 0
    lax.fori_loop(0, n // 256, drain, 0)


def child_call(n, m, land, groups, side):
    dma = pltpu.SemaphoreType.DMA
    stages = n // 128
    vmem = pl.BlockSpec(memory_space=pltpu.VMEM)
    return pl.pallas_call(
        functools.partial(child_kernel, n, m, land, groups, side),
        out_shape=[jax.ShapeDtypeStruct((n // groups, n), F32), jax.ShapeDtypeStruct((m, n), F32),
                   jax.ShapeDtypeStruct((m, land * groups), F32)],
        in_specs=[pl.BlockSpec(memory_space=pl.ANY), vmem, vmem],
        out_specs=[vmem] * 3,
        scratch_shapes=[
            pltpu.VMEM((n // 256, n, 256), F32), pltpu.VMEM((stages, land * groups, 128), F32),
            dma((n // 256,)), dma((n // 256, groups)), dma((n // 256, side - 1)), dma((n // 256, side, side - 1)),
            dma((stages, groups)), dma((side - 1,)), dma((side, side - 1)),
        ] + chol_scratch(n, m),
        compiler_params=pltpu.CompilerParams(vmem_limit_bytes=62 << 20, collective_id=0, has_side_effects=True),
    )


def sent_and_summed(array, axis):
    pieces = array.reshape(lax.axis_size(axis), -1, array.shape[1])
    arrived = lax.all_to_all(pieces, axis, split_axis=0, concat_axis=0, tiled=True)
    return arrived.sum(axis=0)


def on_device(child_pivot, child_coupling, parent_arrow, row_map, block_pattern):
    own_rows = child_pivot[0]
    parent_index = row_map[0]
    row_count, pivot_count = own_rows.shape
    parent_count, pivots = parent_arrow.shape
    front_index = lax.axis_index("front")
    front_groups = lax.axis_size("front")
    slot_index = (
        parent_index // parent_count // front_groups * parent_count + parent_index % parent_count
    )
    spread_rows = lax.axis_size("bulk") * parent_count
    routing = (slot_index[:, None] == jnp.arange(spread_rows)[None, :]).astype(F32)
    hits = routing[:, :parent_count].T.astype(BF)
    lower_rows, coupling, reached = child_call(pivot_count, row_count, parent_count, front_groups, 4)(
        own_rows, child_coupling[0], hits
    )
    routed = jnp.dot(routing.T, reached, precision=HIGHEST_PRECISION)
    device_index = lax.axis_index("bulk") * front_groups + front_index
    first_row = device_index * parent_count
    block_rows = (first_row + jnp.arange(parent_count)) // BLOCK
    picker = (block_rows[:, None] == jnp.arange(block_pattern.shape[0])[None, :]).astype(F32)
    row_mask = jnp.dot(picker, block_pattern.astype(F32), precision=HIGHEST_PRECISION)
    masked = parent_arrow * jnp.repeat(row_mask, BLOCK, axis=1)
    top = routed[:parent_count] + jnp.where(lax.axis_index("bulk") == 0, masked, 0.0)
    top = lax.psum(top, "bulk")
    pivot_block = lax.all_gather(top, "front", axis=0, tiled=True)
    assembled = masked + sent_and_summed(routed, "bulk")
    factor_rows, solved = parent_call(pivots, parent_count)(pivot_block, assembled)
    parent_rows = jnp.where(first_row < pivots, factor_rows, solved)
    return (lower_rows[None], coupling[None], parent_rows)


def solution(mesh):
    placed = (
        P("bulk", "front", None),
        P("bulk", "front", None),
        P(("bulk", "front"), None),
        P("bulk", "front"),
        P(),
    )
    return jax.shard_map(
        on_device,
        mesh=mesh,
        in_specs=placed,
        out_specs=(P("bulk", "front", None), P("bulk", "front", None), P(("bulk", "front"), None)),
        check_vma=False,
    )
```

time: 525 us -> 447 us (0.85)
  waiting for transfers between devices: 324 us -> 137 us
  Pallas kernels: 163 us -> 269 us
  matrix products: 13.2 us -> 3.59 us
  starting transfers between devices: 5.25 us -> 14.5 us
    all_gather x2 -> x0, waiting for transfers between devices: 186 us -> none  [the longest x1 116 us: on_device(): child_whole = lax.all_gather(own_rows, 'front', axis=0, tiled=True)]
    pallas_call x2, Pallas kernels: 163 us -> 269 us  [the longest x1 225 us: on_device(): child_call(pivot_count, row_count, parent_count, front_groups, 4)]
    dot_general x2 -> x0, matrix products: 10.5 us -> none  [the longest x1 7.96 us: on_device(): reached = -jnp.dot(coupling, landing.T, precision=lax.Precision.HIGH)]
    all_to_all x1, starting transfers between devices: 5.13 us -> 14.5 us  [sent_and_summed(): lax.all_to_all(pieces, axis, split_axis=0, concat_axis=0, tiled=True)]
  transfers between devices with their start and end apart: 5 -> 3, of which waited for: 5 -> 3; matrix products, arithmetic and copies ran while one was open for 0% -> 0% of each run, Pallas kernels for 0% -> 0%
where the time goes in v2:
time: 447 us
  Pallas kernels  269 us (60%)
  waiting for transfers between devices  137 us (31%)
  starting transfers between devices  14.5 us (3%)
  between operations  14.1 us (3%)
    pallas_call x1, Pallas kernels, on_device(): child_call(pivot_count, row_count, parent_count, front_groups, 4)  225 us
    psum x1, waiting for transfers between devices, on_device(): top = lax.psum(top, 'bulk')  56.1 us
    all_gather x1, waiting for transfers between devices, on_device(): pivot_block = lax.all_gather(top, 'front', axis=0, tiled=True)  54.7 us
    pallas_call x1, Pallas kernels, on_device(): parent_call(pivots, parent_count)(pivot_block, assembled)  44.5 us
    all_to_all x1, waiting for transfers between devices, sent_and_summed(): lax.all_to_all(pieces, axis, split_axis=0, concat_axis=0, tiled=True)  26 us
    all_to_all x1, starting transfers between devices, sent_and_summed(): lax.all_to_all(pieces, axis, split_axis=0, concat_axis=0, tiled=True)  14.5 us
  transfers between devices with their start and end apart: 3, of which 3 were waited for; matrix products, arithmetic and copies ran while one was open for 0% of the time, Pallas kernels for 0%

profile of v2, /device:TPU:1, one launch (start us, length us, event | category | flops | bytes accessed | tf_op | source)
XLA Modules:
  0.0 446.7 jit_solution(16220962458336539918)
XLA Ops:
  7.2 0.7 fusion.6
  7.9 0.6 fusion.2.hit_ref
  8.5 224.9 %shard_map.76 = (f32[128,2048]{1,0:T(8,128)}, f32[128,2048]{1,0:T(8,128)}, f32[128,1024]{1,0:T(8,128)}) custom-call(f32[128,2048]{1,0:T(8,128)} %bitcast.28, f32[128,2048]{1,0:T(8,128)} %bitcast.29, bf16[64,128]{1,0:T(8,128)(2,1)} %fusion.2.hit_ref), custom_call_target="tpu_custom_call" | custom-call | tf_op jit(solution)/shard_map/pallas_call | solution.py:441
  233.4 3.4 fusion.4
  236.8 0.0 copy-start.4
  236.8 14.5 %all-to-all-start = ((f32[8,64,1024]{2,1,0:T(8,128)}), f32[8,64,1024]{2,1,0:T(8,128)S(1)}, u32[]{:S(2)}, u32[]{:S(2)}) async-start(f32[8,64,1024]{2,1,0:T(8,128)} %bitcast.6), calls=%async_computation | async-start | bytes 4194304 | tf_op jit(solution)/shard_map/all_to_all | solution.py:424
  251.3 0.0 copy-start.3
  251.3 0.0 all-reduce.2.cloned.1.call-start
  251.3 0.0 copy-done.4
  251.3 0.2 fusion.1
  251.5 26.0 %all-to-all-done = f32[8,64,1024]{2,1,0:T(8,128)S(1)} async-done(((f32[8,64,1024]{2,1,0:T(8,128)}), f32[8,64,1024]{2,1,0:T(8,128)S(1)}, u32[]{:S(2)}, u32[]{:S(2)}) %all-to-all-start) | async-done | bytes 2097184 | tf_op jit(solution)/shard_map/all_to_all | solution.py:424
  277.5 0.1 reduce_sum.9
  277.6 0.1 broadcast_in_dim.19
  277.8 0.0 copy-done.3
  277.8 1.8 fusion
  279.6 0.0 all-reduce.2.cloned.1.call-update
  279.6 0.0 all-gather.2.cloned.1.call-start
  279.6 56.1 %all-reduce.2.cloned.1.call-done = f32[64,1024]{1,0:T(8,128)} async-done(((f32[64,1024]{1,0:T(8,128)}), f32[64,1024]{1,0:T(8,128)}) %all-reduce.2.cloned.1.call-update) | async-done | bytes 262160 | tf_op jit(solution)/shard_map/psum | solution.py:452
  335.8 0.0 all-gather.2.cloned.1.call-update
  335.8 54.7 %all-gather.2.cloned.1.call-done.a_ref = f32[1024,1024]{1,0:T(8,128)} async-done(((f32[64,1024]{1,0:T(8,128)}), f32[1024,1024]{1,0:T(8,128)}) %all-gather.2.cloned.1.call-update) | async-done | bytes 4194320 | tf_op jit(solution)/shard_map/all_gather | solution.py:453
  390.5 0.0 copy-start
  390.5 2.2 copy-done
  392.7 0.0 copy-start.2
  392.7 44.5 %shard_map.77 = (f32[64,1024]{1,0:T(8,128)S(1)}, f32[64,1024]{1,0:T(8,128)S(1)}) custom-call(f32[1024,1024]{1,0:T(8,128)S(1)} %copy-done, f32[64,1024]{1,0:T(8,128)S(1)} %get-tuple-element.13.c_ref), custom_call_target="tpu_custom_call" | custom-call | tf_op jit(solution)/shard_map/pallas_call | solution.py:455
  437.2 0.0 copy-start.1
  437.2 0.7 broadcast_select_fusion
  437.9 0.0 copy-done.2
  437.9 1.0 copy.19
  438.9 0.0 copy-done.1
  438.9 1.0 copy.20
  (2 shorter events, 0.1 us)
Async XLA Ops:
  236.8 14.5 %copy-start.4 = (s32[64,8]{0,1:T(8,128)S(1)}, s32[64,8]{0,1:T(8,128)}, u32[]{:S(2)}) copy-start(s32[64,8]{0,1:T(8,128)} %param.9) | copy-start | bytes 6148
  236.8 40.7 %all-to-all-start = ((f32[8,64,1024]{2,1,0:T(8,128)}), f32[8,64,1024]{2,1,0:T(8,128)S(1)}, u32[]{:S(2)}, u32[]{:S(2)}) async-start(f32[8,64,1024]{2,1,0:T(8,128)} %bitcast.6), calls=%async_computation | async-start | bytes 4194304 | tf_op jit(solution)/shard_map/all_to_all | solution.py:424
  251.3 26.5 %copy-start.3 = (f32[64,1024]{1,0:T(8,128)S(1)}, f32[64,1024]{1,0:T(8,128)}, u32[]{:S(2)}) copy-start(f32[64,1024]{1,0:T(8,128)} %param.7) | copy-start | bytes 786436
  251.3 84.5 %all-reduce.2.cloned.1.call-start = ((), (), s32[]{:S(2)}) async-start(), calls=%async_computation.1 | async-start | bytes 524288 | tf_op jit(solution)/shard_map/psum | solution.py:452
  279.6 110.9 %all-gather.2.cloned.1.call-start = ((), (), s32[]{:S(2)}) async-start(), calls=%async_computation.2 | async-start | bytes 4456448 | tf_op jit(solution)/shard_map/all_gather | solution.py:453
  390.5 2.2 copy-start
  392.7 45.2 %copy-start.2 = (f32[128,2048]{1,0:T(8,128)S(1)}, f32[128,2048]{1,0:T(8,128)}, u32[]{:S(2)}) copy-start(f32[128,2048]{1,0:T(8,128)} %get-tuple-element.8) | copy-start | bytes 3145732
  437.2 1.7 copy-start.1
Sparse Core Ops, SparseCore 0:
  279.7 56.0 all-reduce.1
  337.9 52.5 all-gather.1

commit v3 on v2

v3 whole, which is shorter than its diff:
```python
import functools

import jax
import jax.numpy as jnp
from jax import lax
from jax.experimental import pallas as pl
from jax.experimental.pallas import tpu as pltpu
from jax.sharding import PartitionSpec as P

BLOCK = 128
F32, BF = jnp.float32, jnp.bfloat16
NT = (((1,), (1,)), ((), ()))
MESH = pl.DeviceIdType.MESH
HIGHEST_PRECISION = lax.Precision.HIGHEST


def factor_block(load_row, store_u, store_e, n=128, sb=8):
    nb = n // sb
    W = [load_row(v) for v in range(nb)]
    lane = lax.broadcasted_iota(jnp.int32, (sb, n), 1)
    sub = lax.broadcasted_iota(jnp.int32, (sb, n), 0)
    for b in range(nb):
        base = b * sb
        inblk = (lane >= base) & (lane < base + sb)
        R = W[b]
        S = [jnp.broadcast_to(R[:, base + j:base + j + 1], (sb, n)) for j in range(sb)]
        F = {}
        for j in range(sb):
            for i in range(j, sb):
                F[i, j] = jnp.broadcast_to(S[j][i:i + 1, :], (sb, n))
        rinv = []
        for j in range(sb):
            r = lax.rsqrt(F[j, j])
            rinv.append(r)
            for i in range(j, sb):
                F[i, j] = F[i, j] * r
            for c in range(j + 1, sb):
                for i in range(c, sb):
                    F[i, c] = F[i, c] - F[i, j] * F[c, j]
        RI = jnp.where(inblk, (lane - base == sub).astype(jnp.float32), R)
        u = []
        for j in range(sb):
            t = jnp.broadcast_to(RI[j:j + 1, :], (sb, n))
            for m in range(j):
                t = t - F[j, m] * u[m]
            u.append(t * rinv[j])
        e = u[0]
        for j in range(1, sb):
            e = jnp.where(sub == j, u[j], e)
        store_e(b, jnp.where(lane < base + sb, e, 0.0))
        d = jnp.zeros((sb, n), jnp.float32)
        for j in range(sb):
            for c in range(j, sb):
                d = jnp.where((sub == j) & (lane == base + c), F[c, j], d)
        store_u(b, jnp.where(inblk, d, jnp.where(lane < base, 0.0, e)))
        for v in range(b + 1, nb):
            C = []
            acc = jnp.where(inblk, 0.0, W[v])
            for j in range(sb):
                c = jnp.broadcast_to(W[v][:, base + j:base + j + 1], (sb, n))
                for m in range(j):
                    c = c - C[m] * F[j, m]
                c = c * rinv[j]
                C.append(c)
                acc = acc - c * u[j]
            W[v] = acc


def split(x):
    hi = x.astype(BF)
    return hi, (x - hi.astype(F32)).astype(BF)

def dot3(ah, al, bh, bl):
    d = functools.partial(lax.dot_general, dimension_numbers=NT, preferred_element_type=F32)
    return d(ah, bh) + (d(ah, bl) + d(al, bh))


def dynamic(p, size):
    return pl.ds(pl.multiple_of(p * size, size), size)


def chol_stage(p, n, m, block, extra, T, Lh, Ll, U, E, Eh, El, *, before, after_factor, before_rest):
    full = n // 256
    k, half = p // 2, p % 2
    prow = pl.multiple_of(p * 128, 128)
    pcol = pl.ds(prow, 128)
    qcol = pl.ds(pl.multiple_of(prow - half * 128, 128), 128)
    hcol = dynamic(half, 128)

    def update(kk, r, cnt):
        rows = pl.ds(r, cnt)
        x = extra(kk) if isinstance(r, int) and r >= n else block(kk, rows)
        if kk:
            kr = pl.ds(256 * kk, 256)
            x = x - dot3(Lh[rows, :256 * kk], Ll[rows, :256 * kk], Lh[kr, :256 * kk], Ll[kr, :256 * kk])
        T[rows, :] = x

    def half_update(r, cnt):
        rows = pl.ds(r, cnt)
        T[rows, 128:256] = T[rows, 128:256] - dot3(Lh[rows, qcol], Ll[rows, qcol], Lh[pcol, qcol], Ll[pcol, qcol])

    def solve(r, cnt):
        rows = pl.ds(r, cnt)
        th, tl = split(T[rows, hcol])
        x = dot3(th, tl, Eh[...], El[...])
        T[rows, hcol] = x
        xh, xl = split(x)
        Lh[rows, pcol] = xh
        Ll[rows, pcol] = xl

    def rest(body):
        def step(r, _):
            body(pl.multiple_of(r * 256, 256), 256)
            return 0
        lax.fori_loop(k + 1, full, step, 0)
        if m:
            body(n, m)

    before(p)
    for kk in range(full):
        @pl.when(p == 2 * kk)
        def _():
            update(kk, 256 * kk, 256)

    @pl.when(half == 1)
    def _():
        half_update(prow, 128)

    def su(b, x): U[pl.ds(8 * b, 8), :] = x
    def se(b, x): E[pl.ds(8 * b, 8), :] = x
    factor_block(lambda v: T[pl.ds(pl.multiple_of(prow + 8 * v, 8), 8), hcol], su, se)
    eh, el = split(E[...])
    Eh[...] = eh
    El[...] = el
    after_factor(p)

    @pl.when(half == 0)
    def _():
        solve(pl.multiple_of(prow + 128, 128), 128)
    before_rest(p)
    for kk in range(full):
        @pl.when(p == 2 * kk)
        def _():
            def both(r, cnt):
                update(kk, r, cnt)
                solve(r, cnt)
            rest(both)

    @pl.when(half == 1)
    def _():
        def both(r, cnt):
            half_update(r, cnt)
            solve(r, cnt)
        rest(both)
    T[pl.ds(prow, 128), hcol] = U[...].T


def put_rows(p, n, m, own, row0, T, l_out, c_out):
    hcol, pcol = dynamic(p % 2, 128), dynamic(p, 128)
    c_out[:, pcol] = T[n:n + m, hcol]
    mine = T[pl.ds(pl.multiple_of(row0, own), own), hcol]
    l_out[:, pcol] = jnp.where(p * 128 < row0 + own, mine, 0.0)


def chol_scratch(n, m):
    return [pltpu.VMEM((n + m, 256), F32), pltpu.VMEM((n + m, n), BF), pltpu.VMEM((n + m, n), BF),
            pltpu.VMEM((128, 128), F32), pltpu.VMEM((128, 128), F32),
            pltpu.VMEM((128, 128), BF), pltpu.VMEM((128, 128), BF)]


def nothing(p):
    pass


def remote(src, dst, send_sem, recv_sem, to):
    return pltpu.make_async_remote_copy(src_ref=src, dst_ref=dst, send_sem=send_sem, recv_sem=recv_sem,
                                        device_id=to, device_id_type=MESH)


def meet(axes):
    barrier = pltpu.get_barrier_semaphore()
    count = 0
    for axis, size in axes:
        here = lax.axis_index(axis)
        for d in range(1, size):
            pl.semaphore_signal(barrier, inc=1, device_id={axis: (here + d) % size}, device_id_type=MESH)
        count += size - 1
    pl.semaphore_wait(barrier, count)


class Square:
    def __init__(self, at, arrive, sems, has, own_ready, once):
        self.at, self.arrive, self.sems, self.has, self.own_ready, self.once = at, arrive, sems, has, own_ready, once
        me = lax.axis_index("front")
        self.me, self.x, self.z = me, me // 4, me % 4
        self.parity = (self.x + self.z) % 2

    def near(self, axis, d):
        along_z = self.x * 4 + (self.z + d) % 4
        along_x = (self.x + d) % 4 * 4 + self.z
        if isinstance(axis, int):
            return along_x if axis else along_z
        return jnp.where(axis == 0, along_z, along_x)

    def copy(self, k, f, part, phase, slot, to, src=None):
        s = 0 if self.once else k
        dst = self.at(k, f, part)
        return remote(dst if src is None else src, dst, self.sems[phase].at[s, slot], self.arrive.at[k, f], {"front": to})

    def arrival(self, k, f):
        return pltpu.make_async_copy(self.at(k, f, None), self.at(k, f, None), self.arrive.at[k, f])

    def plan(self, phase):
        x, z = self.x, self.z
        if phase == 0:
            return [(self.me, None, 0, self.near(self.parity, 1)), (self.me, None, 1, self.near(self.parity, 3))]
        if phase == 1:
            r = 1 - self.parity
            return [(self.near(r, 3), 0, 0, self.near(r, 1)), (self.near(r, 1), 1, 1, self.near(r, 3))]
        out = []
        if phase == 2:
            for j in range(2):
                f = x * 4 + x % 2 + 2 * j
                g = ((z + 1) % 2 + 2 * j) * 4 + z
                for d, i in ((1, 0), (3, 1)):
                    out.append((f, None, 4 * j + i, self.near(1, d)))
                for d, i in ((1, 2), (3, 3)):
                    out.append((g, None, 4 * j + i, self.near(0, d)))
            return out
        for j in range(2):
            for d, part in ((3, 0), (1, 1)):
                back = 4 - d
                xs, zs = (x + d) % 4, (z + d) % 4
                out.append((xs * 4 + xs % 2 + 2 * j, part, 4 * j + part, self.near(1, back)))
                out.append((((zs + 1) % 2 + 2 * j) * 4 + zs, part, 4 * j + 2 + part, self.near(0, back)))
        return out

    def start(self, phase, k, src=None):
        seen = None
        for f, part, slot, to in self.plan(phase):
            new = f is not seen
            seen = f

            @pl.when(self.has(k, f))
            def _():
                if new and phase in (1, 3):
                    self.arrival(k, f).wait()
                if new and phase == 2:
                    @pl.when(f == self.me)
                    def _():
                        self.own_ready(k)

                    @pl.when((f == self.near(0, 2)) | (f == self.near(1, 2)))
                    def _():
                        self.arrival(k, f).wait()
                if self.once:
                    @pl.when(k > 0)
                    def _():
                        self.copy(k - 1, f, part, phase, slot, to, src).wait_send()
                self.copy(k, f, part, phase, slot, to, src).start()

    def finish(self, k, lo, hi):
        for j in range(2):
            xs, zs = (self.x + 2) % 4, (self.z + 2) % 4
            for f in (xs * 4 + xs % 2 + 2 * j, ((zs + 1) % 2 + 2 * j) * 4 + zs):
                @pl.when(self.has(k, f) & (f >= lo) & (f < hi))
                def _():
                    self.arrival(k, f).wait()

    def prologue(self, first):
        first(0)
        self.start(1, 0)
        first(1)
        self.start(2, 0)
        self.start(1, 1)
        first(2)
        self.start(3, 0)
        self.start(2, 1)
        self.start(1, 2)
        first(3)

    def ahead(self, s, wide, first):
        j = s // 3

        @pl.when(s % 3 == 0)
        def _():
            @pl.when(j + 2 < wide)
            def _():
                self.start(2, j + 2)

            @pl.when(j + 3 < wide)
            def _():
                self.start(1, j + 3)

            @pl.when(j + 4 < wide)
            def _():
                first(j + 4)

        @pl.when((s % 3 == 1) & (j + 1 < wide))
        def _():
            self.start(3, j + 1)

    def drain(self, k, src=None):
        for phase in range(4):
            for f, part, slot, to in self.plan(phase):
                @pl.when(self.has(k, f))
                def _():
                    self.copy(k, f, part, phase, slot, to, src if phase == 0 else None).wait_send()


def square_sems(n):
    return [pltpu.SemaphoreType.DMA((n, c)) for c in (2, 2, 8, 8)]


def child_kernel(n, m, land, groups, a_ref, c_ref, hit_ref, l_out, c_out, reach, G, LG, own_sem, arrive, land_arrive, *more):
    sems, land_sems, scratch = more[:4], more[4:8], more[8:]
    T, Lh, Ll = scratch[0], scratch[1], scratch[2]
    stages, rows_own, wide = n // 128, n // groups, n // 256
    me = lax.axis_index("front")
    meet((("front", groups),))

    def part_of(ref, k, f, size, part):
        if part is None:
            return ref.at[k, dynamic(f, size), :]
        return ref.at[k, dynamic(2 * f + part, size // 2), :]

    def own_copy(k):
        return pltpu.make_async_copy(a_ref.at[:, dynamic(k, 256)], G.at[k, dynamic(me, rows_own), :], own_sem.at[k])

    def has(k, f):
        return f // 2 >= k
    rows = Square(lambda k, f, part: part_of(G, k, f, rows_own, part), arrive, sems, has, lambda k: own_copy(k).wait(), False)
    lands = Square(lambda k, f, part: part_of(LG, k, f, land, part), land_arrive, land_sems,
                   lambda k, f: f >= 0, nothing, True)

    def first(k):
        rows.start(0, k, a_ref.at[:, dynamic(k, 256)])

        @pl.when(has(k, me))
        def _():
            own_copy(k).start()

    def land_use(p):
        lands.finish(p, 0, groups)
        pcol = dynamic(p, 128)
        gh, gl = split(LG[p])
        reach[...] = reach[...] - dot3(Lh[n:n + m, pcol], Ll[n:n + m, pcol], gh, gl)

    def catch_up(p, late, long, short, body):
        def upto(q):
            return jnp.where(q >= late, q - short, q - long)

        def step(q, _):
            body(q)
            return 0
        lax.fori_loop(jnp.maximum(upto(p - 1) + 1, 0), jnp.maximum(upto(p) + 1, 0), step, 0)

    rows.prologue(first)
    reach[...] = jnp.zeros_like(reach)

    def before(p):
        @pl.when(p % 2 == 0)
        def _():
            rows.finish(p // 2, p, p + 2)

    def after_factor(p):
        rows.ahead(2 * p, wide, first)
        catch_up(p, 11, 2, 1, lambda q: lands.start(1, q))
        catch_up(p, 12, 5, 2, lambda q: lands.start(3, q))

    def before_rest(p):
        @pl.when(p % 2 == 0)
        def _():
            rows.finish(p // 2, p + 2, groups)

    def stage(p, _):
        chol_stage(
            p, n, m,
            lambda kk, rows: G[kk, rows, :],
            lambda kk: c_ref[:, 256 * kk:256 * kk + 256],
            *scratch, before=before, after_factor=after_factor, before_rest=before_rest,
        )
        pcol = dynamic(p, 128)
        nn = functools.partial(jnp.dot, preferred_element_type=F32)
        LG[p, dynamic(me, land), :] = nn(hit_ref[...], Lh[n:n + m, pcol]) + nn(hit_ref[...], Ll[n:n + m, pcol])
        put_rows(p, n, m, rows_own, me * rows_own, T, l_out, c_out)

        rows.ahead(2 * p + 1, wide, first)
        catch_up(p, 11, 3, 1, lambda q: lands.start(2, q))
        catch_up(p, 12, 6, 3, land_use)
        lands.start(0, p)
        return 0
    lax.fori_loop(0, stages, stage, 0)
    last = stages - 1
    lands.start(3, last - 1)
    lands.start(1, last)
    land_use(last - 2)
    lands.start(2, last)
    land_use(last - 1)
    lands.start(3, last)
    land_use(last)
    lands.drain(last)

    def drain(k, _):
        rows.drain(k, a_ref.at[:, dynamic(k, 256)])
        return 0
    lax.fori_loop(0, wide, drain, 0)


def child_call(n, m, land, groups, side):
    dma = pltpu.SemaphoreType.DMA
    stages = n // 128
    vmem = pl.BlockSpec(memory_space=pltpu.VMEM)
    return pl.pallas_call(
        functools.partial(child_kernel, n, m, land, groups),
        out_shape=[jax.ShapeDtypeStruct((n // groups, n), F32), jax.ShapeDtypeStruct((m, n), F32),
                   jax.ShapeDtypeStruct((m, land * groups), F32)],
        in_specs=[pl.BlockSpec(memory_space=pl.ANY), vmem, vmem],
        out_specs=[vmem] * 3,
        scratch_shapes=[
            pltpu.VMEM((n // 256, n, 256), F32), pltpu.VMEM((stages, land * groups, 128), F32),
            dma((n // 256,)), dma((n // 256, groups)), dma((stages, groups)),
        ] + square_sems(n // 256) + square_sems(1) + chol_scratch(n, m),
        compiler_params=pltpu.CompilerParams(vmem_limit_bytes=62 << 20, collective_id=0, has_side_effects=True),
    )


def parent_kernel(n, m, groups, bulks, reach, route, masked, out, PV, TP, RS, SB, RB, XH, XL, EH, EL,
                  scatter_send, scatter_come, gather_send, gather_come, spread_send, spread_come, arrive, *more):
    sems, scratch = more[:4], more[4:]
    T, Lh, Ll, U, E, Eh, El = scratch
    wide, full = n // 256, n // 128
    me, here = lax.axis_index("front"), lax.axis_index("bulk")
    meet((("front", groups), ("bulk", bulks)))
    nn = functools.partial(jnp.dot, preferred_element_type=F32)
    rh, rl = split(reach[...])

    def slot(b):
        r = route[b * m:(b + 1) * m, :]
        return nn(r, rh) + nn(r, rl)

    def other(d):
        return (here + d) % bulks

    def needed(j):
        return j // 2 <= me // 4

    def scatter(d):
        j = other(d)
        return remote(TP.at[j], RS.at[here], scatter_send.at[d - 1], scatter_come.at[here], {"bulk": j})

    def scattered(b):
        return pltpu.make_async_copy(RS.at[b], RS.at[b], scatter_come.at[b])

    def piece(j):
        return PV.at[j // 2, dynamic(me, m), dynamic(j % 2, 128)]

    def gather(d):
        return remote(piece(here), piece(here), gather_send.at[d - 1], gather_come.at[here], {"bulk": other(d)})

    def spread(d):
        b = other(d)
        return remote(SB.at[b], RB.at[here], spread_send.at[d - 1], spread_come.at[here], {"bulk": b})

    def spreaded(b):
        return pltpu.make_async_copy(RB.at[b], RB.at[b], spread_come.at[b])

    top = slot(0) + jnp.where(here == 0, masked[...], 0.0)
    for j in range(full):
        TP[j] = top[:, 128 * j:128 * j + 128]
    for d in range(1, bulks):
        @pl.when(needed(other(d)))
        def _():
            scatter(d).start()
    for b in range(1, bulks):
        SB[b] = slot(b)

    @pl.when(needed(here))
    def _():
        RS[here] = TP[here]
        for d in range(1, bulks):
            scattered(other(d)).wait()
        total = RS[0]
        for b in range(1, bulks):
            total = total + RS[b]
        PV[here // 2, dynamic(me, m), dynamic(here % 2, 128)] = total
        for d in range(1, bulks):
            gather(d).start()
    for d in range(1, bulks):
        j = other(d)

        @pl.when(needed(j))
        def _():
            pltpu.make_async_copy(piece(j), piece(j), gather_come.at[j]).wait()

    def part_at(k, f, part):
        if part is None:
            return PV.at[k, dynamic(f, m), :]
        return PV.at[k, dynamic(2 * f + part, m // 2), :]
    rows = Square(part_at, arrive, sems, lambda k, f: f // 4 >= k, nothing, False)

    def first(k):
        rows.start(0, k)
    first(0)
    for d in range(1, bulks):
        @pl.when(other(d) != 0)
        def _():
            spread(d).start()
    rows.start(1, 0)
    first(1)
    rows.start(2, 0)
    rows.start(1, 1)
    first(2)
    rows.start(3, 0)
    rows.start(2, 1)
    rows.start(1, 2)
    first(3)

    def before(p):
        @pl.when(p % 2 == 0)
        def _():
            rows.finish(p // 2, 2 * p, 2 * p + 4)

    def before_rest(p):
        @pl.when(p % 2 == 0)
        def _():
            rows.finish(p // 2, 2 * p + 4, groups)

    def stage(p, _):
        chol_stage(p, n, 0, lambda kk, r: PV[kk, r, :], None, *scratch, before=before,
                   after_factor=lambda p: rows.ahead(2 * p, wide, first), before_rest=before_rest)
        EH[p] = Eh[...]
        EL[p] = El[...]
        mine = T[dynamic(me, m), dynamic(p % 2, 128)]
        out[:, dynamic(p, 128)] = jnp.where(p * 128 < (me + 1) * m, mine, 0.0)
        rows.ahead(2 * p + 1, wide, first)
        return 0
    lax.fori_loop(0, full, stage, 0)

    @pl.when(here != 0)
    def _():
        for d in range(1, bulks):
            spreaded(other(d)).wait()
        RB[here] = SB[here]
        x = masked[...]
        for b in range(bulks):
            x = x + RB[b]
        for p in range(full):
            cols = slice(128 * p, 128 * p + 128)
            y = x[:, cols]
            if p:
                y = y - dot3(XH[:, :128 * p], XL[:, :128 * p], Lh[cols, :128 * p], Ll[cols, :128 * p])
            yh, yl = split(y)
            y = dot3(yh, yl, EH[p], EL[p])
            out[:, cols] = y
            yh, yl = split(y)
            XH[:, cols] = yh
            XL[:, cols] = yl
    for d in range(1, bulks):
        @pl.when(needed(other(d)))
        def _():
            scatter(d).wait_send()

        @pl.when(needed(here))
        def _():
            gather(d).wait_send()

        @pl.when(other(d) != 0)
        def _():
            spread(d).wait_send()

    def drain(k, _):
        rows.drain(k)
        return 0
    lax.fori_loop(0, wide, drain, 0)


def parent_call(n, m, groups, bulks):
    dma = pltpu.SemaphoreType.DMA
    vmem = pl.BlockSpec(memory_space=pltpu.VMEM)
    full, wide = n // 128, n // 256
    return pl.pallas_call(
        functools.partial(parent_kernel, n, m, groups, bulks),
        out_shape=jax.ShapeDtypeStruct((m, n), F32),
        in_specs=[vmem] * 3,
        out_specs=vmem,
        scratch_shapes=[
            pltpu.VMEM((wide, n, 256), F32), pltpu.VMEM((full, m, 128), F32), pltpu.VMEM((bulks, m, 128), F32),
            pltpu.VMEM((bulks, m, n), F32), pltpu.VMEM((bulks, m, n), F32), pltpu.VMEM((m, n), BF), pltpu.VMEM((m, n), BF),
            pltpu.VMEM((full, 128, 128), BF), pltpu.VMEM((full, 128, 128), BF),
            dma((bulks - 1,)), dma((bulks,)), dma((bulks - 1,)), dma((bulks,)), dma((bulks - 1,)), dma((bulks,)),
            dma((wide, groups)),
        ] + square_sems(wide) + chol_scratch(n, 0),
        compiler_params=pltpu.CompilerParams(vmem_limit_bytes=40 << 20, collective_id=1, has_side_effects=True),
    )


def on_device(child_pivot, child_coupling, parent_arrow, row_map, block_pattern):
    own_rows = child_pivot[0]
    parent_index = row_map[0]
    row_count, pivot_count = own_rows.shape
    parent_count, pivots = parent_arrow.shape
    front_index = lax.axis_index("front")
    front_groups = lax.axis_size("front")
    slot_index = (
        parent_index // parent_count // front_groups * parent_count + parent_index % parent_count
    )
    spread_rows = lax.axis_size("bulk") * parent_count
    routing = (jnp.arange(spread_rows)[:, None] == slot_index[None, :]).astype(BF)
    lower_rows, coupling, reached = child_call(pivot_count, row_count, parent_count, front_groups, 4)(
        own_rows, child_coupling[0], routing[:parent_count]
    )
    device_index = lax.axis_index("bulk") * front_groups + front_index
    first_row = device_index * parent_count
    block_rows = (first_row + jnp.arange(parent_count)) // BLOCK
    picker = (block_rows[:, None] == jnp.arange(block_pattern.shape[0])[None, :]).astype(F32)
    row_mask = jnp.dot(picker, block_pattern.astype(F32), precision=HIGHEST_PRECISION)
    masked = parent_arrow * jnp.repeat(row_mask, BLOCK, axis=1)
    parent_rows = parent_call(pivots, parent_count, front_groups, lax.axis_size("bulk"))(reached, routing, masked)
    return (lower_rows[None], coupling[None], parent_rows)


def solution(mesh):
    placed = (
        P("bulk", "front", None),
        P("bulk", "front", None),
        P(("bulk", "front"), None),
        P("bulk", "front"),
        P(),
    )
    return jax.shard_map(
        on_device,
        mesh=mesh,
        in_specs=placed,
        out_specs=(P("bulk", "front", None), P("bulk", "front", None), P(("bulk", "front"), None)),
        check_vma=False,
    )
```

time: 447 us -> 283 us (0.63)
  waiting for transfers between devices: 137 us -> 0 us
  starting transfers between devices: 14.5 us -> 0 us
  between operations: 14.1 us -> 0.75 us
  Pallas kernels: 269 us -> 274 us
    psum x1 -> x0, waiting for transfers between devices: 56.1 us -> none  [on_device(): top = lax.psum(top, 'bulk')]
    all_gather x1 -> x0, waiting for transfers between devices: 54.7 us -> none  [on_device(): pivot_block = lax.all_gather(top, 'front', axis=0, tiled=True)]
    pallas_call x1, Pallas kernels: 44.5 us -> 87.5 us  [on_device(): parent_call(pivots, parent_count, front_groups, lax.axis_size('bulk'))]
    pallas_call x1, Pallas kernels: 225 us -> 186 us  [on_device(): child_call(pivot_count, row_count, parent_count, front_groups, 4)]
    all_to_all x1 -> x0, waiting for transfers between devices: 26 us -> none  [sent_and_summed(): lax.all_to_all(pieces, axis, split_axis=0, concat_axis=0, tiled=True)]
    all_to_all x1 -> x0, starting transfers between devices: 14.5 us -> none  [sent_and_summed(): lax.all_to_all(pieces, axis, split_axis=0, concat_axis=0, tiled=True)]
  transfers between devices with their start and end apart: 3 -> 0, of which waited for: 3 -> 0; matrix products, arithmetic and copies ran while one was open for 0% -> 0% of each run, Pallas kernels for 0% -> 0%
where the time goes in v3:
time: 283 us; the launch traced here: 280 us
  Pallas kernels  274 us (97%)
  local copies, waits for them, and re-layouts  5.69 us (2%)
    pallas_call x1, Pallas kernels, on_device(): child_call(pivot_count, row_count, parent_count, front_groups, 4)  186 us
    pallas_call x1, Pallas kernels, on_device(): parent_call(pivots, parent_count, front_groups, lax.axis_size('bulk'))  87.5 us

profile of v3, /device:TPU:1, one launch (start us, length us, event | category | flops | bytes accessed | tf_op | source)
XLA Modules:
  0.0 280.3 jit_solution(17912675404622802120)
XLA Ops:
  0.6 0.0 copy-start.4
  0.7 0.0 copy-start.5
  0.7 0.6 copy-done.5
  1.3 0.0 copy-start.3
  1.3 0.0 copy-done.4
  1.4 0.2 fusion.1
  1.6 0.6 slice.4.hit_ref
  2.2 0.1 broadcast_in_dim.15
  2.3 0.0 copy-done.3
  2.4 0.1 bitcast_multiply_fusion.masked
  2.4 186.0 %shard_map.76 = (f32[128,2048]{1,0:T(8,128)}, f32[128,2048]{1,0:T(8,128)}, f32[128,1024]{1,0:T(8,128)}) custom-call(f32[128,2048]{1,0:T(8,128)} %bitcast.10, f32[128,2048]{1,0:T(8,128)} %bitcast.11, bf16[64,128]{1,0:T(8,128)(2,1)} %slice.4.hit_ref), custom_call_target="tpu_custom_call" | custom-call | tf_op jit(solution)/shard_map/pallas_call | solution.py:610
  188.4 0.0 copy-start
  188.5 1.0 copy-done
  189.5 0.0 copy-start.2
  189.5 87.5 %shard_map.77 = f32[64,1024]{1,0:T(8,128)S(1)} custom-call(f32[128,1024]{1,0:T(8,128)S(1)} %copy-done, bf16[512,128]{1,0:T(8,128)(2,1)S(1)} %fusion.route, f32[64,1024]{1,0:T(8,128)S(1)} %bitcast_multiply_fusion.masked), custom_call_target="tpu_custom_call" | custom-call | tf_op jit(solution)/shard_map/pallas_call | solution.py:619
  277.0 0.0 copy-done.2
  277.1 0.0 copy-start.1
  277.1 1.0 copy.15
  278.0 0.6 copy-done.1
  278.7 1.0 copy.16
  279.6 0.7 copy.17
  (3 shorter events, 0.1 us)
Async XLA Ops:
  0.6 0.7 copy-start.4
  0.7 0.7 copy-start.5
  1.3 1.0 copy-start.3
  188.4 1.0 copy-start
  189.5 87.6 %copy-start.2 = (f32[128,2048]{1,0:T(8,128)S(1)}, f32[128,2048]{1,0:T(8,128)}, u32[]{:S(2)}) copy-start(f32[128,2048]{1,0:T(8,128)} %get-tuple-element.6) | copy-start | bytes 3145732
  277.1 1.6 copy-start.1

commit v4 on v3

--- a/solution.py
+++ b/solution.py
@@ -79,7 +79,19 @@
     return pl.ds(pl.multiple_of(p * size, size), size)
 
 
-def chol_stage(p, n, m, block, extra, T, Lh, Ll, U, E, Eh, El, *, before, after_factor, before_rest):
+def stack(ref, bh, bl):
+    ref[0:128, 0:128] = bh
+    ref[0:128, 128:256] = bh
+    ref[128:256, 0:128] = bl
+    ref[128:256, 128:256] = jnp.zeros_like(bl)
+
+
+def dot_stacked(ah, al, ref):
+    y = lax.dot_general(jnp.concatenate([ah, al], axis=1), ref[...], NT, preferred_element_type=F32)
+    return y[:, :128] + y[:, 128:]
+
+
+def chol_stage(p, n, m, block, extra, T, Lh, Ll, U, E, ES, LS, *, before, after_factor, before_rest):
     full = n // 256
     k, half = p // 2, p % 2
     prow = pl.multiple_of(p * 128, 128)
@@ -97,22 +109,28 @@
 
     def half_update(r, cnt):
         rows = pl.ds(r, cnt)
-        T[rows, 128:256] = T[rows, 128:256] - dot3(Lh[rows, qcol], Ll[rows, qcol], Lh[pcol, qcol], Ll[pcol, qcol])
+        T[rows, 128:256] = T[rows, 128:256] - dot_stacked(Lh[rows, qcol], Ll[rows, qcol], LS)
 
     def solve(r, cnt):
         rows = pl.ds(r, cnt)
         th, tl = split(T[rows, hcol])
-        x = dot3(th, tl, Eh[...], El[...])
+        x = dot_stacked(th, tl, ES)
         T[rows, hcol] = x
         xh, xl = split(x)
         Lh[rows, pcol] = xh
         Ll[rows, pcol] = xl
 
-    def rest(body):
-        def step(r, _):
-            body(pl.multiple_of(r * 256, 256), 256)
+    def rest(first, body):
+        count = full - first
+
+        def step(i, _):
+            body(pl.multiple_of(first * 256 + i * 512, 256), 512)
             return 0
-        lax.fori_loop(k + 1, full, step, 0)
+        lax.fori_loop(0, count // 2, step, 0)
+        if not isinstance(first, int):
+            pl.when(count % 2 == 1)(lambda: body(n - 256, 256))
+        elif count % 2:
+            body(n - 256, 256)
         if m:
             body(n, m)
 
@@ -124,14 +142,13 @@
 
     @pl.when(half == 1)
     def _():
+        stack(LS, Lh[pcol, qcol], Ll[pcol, qcol])
         half_update(prow, 128)
 
     def su(b, x): U[pl.ds(8 * b, 8), :] = x
     def se(b, x): E[pl.ds(8 * b, 8), :] = x
     factor_block(lambda v: T[pl.ds(pl.multiple_of(prow + 8 * v, 8), 8), hcol], su, se)
-    eh, el = split(E[...])
-    Eh[...] = eh
-    El[...] = el
+    stack(ES, *split(E[...]))
     after_factor(p)
 
     @pl.when(half == 0)
@@ -144,14 +161,14 @@
             def both(r, cnt):
                 update(kk, r, cnt)
                 solve(r, cnt)
-            rest(both)
+            rest(kk + 1, both)
 
     @pl.when(half == 1)
     def _():
         def both(r, cnt):
             half_update(r, cnt)
             solve(r, cnt)
-        rest(both)
+        rest(k + 1, both)
     T[pl.ds(prow, 128), hcol] = U[...].T
 
 
@@ -165,7 +182,7 @@
 def chol_scratch(n, m):
     return [pltpu.VMEM((n + m, 256), F32), pltpu.VMEM((n + m, n), BF), pltpu.VMEM((n + m, n), BF),
             pltpu.VMEM((128, 128), F32), pltpu.VMEM((128, 128), F32),
-            pltpu.VMEM((128, 128), BF), pltpu.VMEM((128, 128), BF)]
+            pltpu.VMEM((256, 256), BF), pltpu.VMEM((256, 256), BF)]
 
 
 def nothing(p):
@@ -194,6 +211,10 @@
         me = lax.axis_index("front")
         self.me, self.x, self.z = me, me // 4, me % 4
         self.parity = (self.x + self.z) % 2
+        self.plans = [self.plan(phase) for phase in range(4)]
+        self.opposite = self.near(0, 2), self.near(1, 2)
+        xs, zs = (self.x + 2) % 4, (self.z + 2) % 4
+        self.final = [f for j in range(2) for f in (xs * 4 + xs % 2 + 2 * j, ((zs + 1) % 2 + 2 * j) * 4 + zs)]
 
     def near(self, axis, d):
         along_z = self.x * 4 + (self.z + d) % 4
@@ -237,11 +258,11 @@
 
     def start(self, phase, k, src=None):
         seen = None
-        for f, part, slot, to in self.plan(phase):
+        for f, part, slot, to in self.plans[phase]:
             new = f is not seen
             seen = f
 
-            @pl.when(self.has(k, f))
+            @self.when(k, f)
             def _():
                 if new and phase in (1, 3):
                     self.arrival(k, f).wait()
@@ -250,7 +271,7 @@
                     def _():
                         self.own_ready(k)
 
-                    @pl.when((f == self.near(0, 2)) | (f == self.near(1, 2)))
+                    @pl.when((f == self.opposite[0]) | (f == self.opposite[1]))
                     def _():
                         self.arrival(k, f).wait()
                 if self.once:
@@ -260,12 +281,15 @@
                 self.copy(k, f, part, phase, slot, to, src).start()
 
     def finish(self, k, lo, hi):
-        for j in range(2):
-            xs, zs = (self.x + 2) % 4, (self.z + 2) % 4
-            for f in (xs * 4 + xs % 2 + 2 * j, ((zs + 1) % 2 + 2 * j) * 4 + zs):
-                @pl.when(self.has(k, f) & (f >= lo) & (f < hi))
-                def _():
-                    self.arrival(k, f).wait()
+        for f in self.final:
+            @pl.when(self.has(k, f) & (f >= lo) & (f < hi) if self.has else True)
+            def _():
+                self.arrival(k, f).wait()
+
+    def when(self, k, f):
+        if self.has:
+            return pl.when(self.has(k, f))
+        return lambda body: body()
 
     def prologue(self, first):
         first(0)
@@ -302,8 +326,8 @@
 
     def drain(self, k, src=None):
         for phase in range(4):
-            for f, part, slot, to in self.plan(phase):
-                @pl.when(self.has(k, f))
+            for f, part, slot, to in self.plans[phase]:
+                @self.when(k, f)
                 def _():
                     self.copy(k, f, part, phase, slot, to, src if phase == 0 else None).wait_send()
 
@@ -331,7 +355,7 @@
         return f // 2 >= k
     rows = Square(lambda k, f, part: part_of(G, k, f, rows_own, part), arrive, sems, has, lambda k: own_copy(k).wait(), False)
     lands = Square(lambda k, f, part: part_of(LG, k, f, land, part), land_arrive, land_sems,
-                   lambda k, f: f >= 0, nothing, True)
+                   None, nothing, True)
 
     def first(k):
         rows.start(0, k, a_ref.at[:, dynamic(k, 256)])
@@ -340,20 +364,20 @@
         def _():
             own_copy(k).start()
 
-    def land_use(p):
-        lands.finish(p, 0, groups)
-        pcol = dynamic(p, 128)
-        gh, gl = split(LG[p])
-        reach[...] = reach[...] - dot3(Lh[n:n + m, pcol], Ll[n:n + m, pcol], gh, gl)
+    def land_use(k):
+        lands.finish(k, 0, groups)
+        cols = dynamic(k, 256)
+        gh, gl = split(LG[k])
+        reach[...] = reach[...] - dot3(Lh[n:n + m, cols], Ll[n:n + m, cols], gh, gl)
 
     def catch_up(p, late, long, short, body):
         def upto(q):
-            return jnp.where(q >= late, q - short, q - long)
+            return jnp.maximum(jnp.where(q >= late, (q - short) // 2, (q - long) // 2) + 1, 0)
 
         def step(q, _):
             body(q)
             return 0
-        lax.fori_loop(jnp.maximum(upto(p - 1) + 1, 0), jnp.maximum(upto(p) + 1, 0), step, 0)
+        lax.fori_loop(upto(p - 1), upto(p), step, 0)
 
     rows.prologue(first)
     reach[...] = jnp.zeros_like(reach)
@@ -365,8 +389,8 @@
 
     def after_factor(p):
         rows.ahead(2 * p, wide, first)
-        catch_up(p, 11, 2, 1, lambda q: lands.start(1, q))
-        catch_up(p, 12, 5, 2, lambda q: lands.start(3, q))
+        catch_up(p, 12, 3, 2, lambda k: lands.start(1, k))
+        catch_up(p, 13, 6, 3, lambda k: lands.start(3, k))
 
     def before_rest(p):
         @pl.when(p % 2 == 0)
@@ -380,23 +404,27 @@
             lambda kk: c_ref[:, 256 * kk:256 * kk + 256],
             *scratch, before=before, after_factor=after_factor, before_rest=before_rest,
         )
-        pcol = dynamic(p, 128)
-        nn = functools.partial(jnp.dot, preferred_element_type=F32)
-        LG[p, dynamic(me, land), :] = nn(hit_ref[...], Lh[n:n + m, pcol]) + nn(hit_ref[...], Ll[n:n + m, pcol])
         put_rows(p, n, m, rows_own, me * rows_own, T, l_out, c_out)
-
+        k = p // 2
+
+        @pl.when(p % 2 == 1)
+        def _():
+            cols = dynamic(k, 256)
+            nn = functools.partial(jnp.dot, preferred_element_type=F32)
+            LG[k, dynamic(me, land), :] = nn(hit_ref[...], Lh[n:n + m, cols]) + nn(hit_ref[...], Ll[n:n + m, cols])
         rows.ahead(2 * p + 1, wide, first)
-        catch_up(p, 11, 3, 1, lambda q: lands.start(2, q))
-        catch_up(p, 12, 6, 3, land_use)
-        lands.start(0, p)
+        catch_up(p, 12, 4, 2, lambda k: lands.start(2, k))
+        catch_up(p, 14, 7, 4, land_use)
+
+        @pl.when(p % 2 == 1)
+        def _():
+            lands.start(0, k)
         return 0
     lax.fori_loop(0, stages, stage, 0)
-    last = stages - 1
-    lands.start(3, last - 1)
+    last = wide - 1
     lands.start(1, last)
-    land_use(last - 2)
+    land_use(last - 1)
     lands.start(2, last)
-    land_use(last - 1)
     lands.start(3, last)
     land_use(last)
     lands.drain(last)
@@ -409,7 +437,6 @@
 
 def child_call(n, m, land, groups, side):
     dma = pltpu.SemaphoreType.DMA
-    stages = n // 128
     vmem = pl.BlockSpec(memory_space=pltpu.VMEM)
     return pl.pallas_call(
         functools.partial(child_kernel, n, m, land, groups),
@@ -418,8 +445,8 @@
         in_specs=[pl.BlockSpec(memory_space=pl.ANY), vmem, vmem],
         out_specs=[vmem] * 3,
         scratch_shapes=[
-            pltpu.VMEM((n // 256, n, 256), F32), pltpu.VMEM((stages, land * groups, 128), F32),
-            dma((n // 256,)), dma((n // 256, groups)), dma((stages, groups)),
+            pltpu.VMEM((n // 256, n, 256), F32), pltpu.VMEM((n // 256, land * groups, 256), F32),
+            dma((n // 256,)), dma((n // 256, groups)), dma((n // 256, groups)),
         ] + square_sems(n // 256) + square_sems(1) + chol_scratch(n, m),
         compiler_params=pltpu.CompilerParams(vmem_limit_bytes=62 << 20, collective_id=0, has_side_effects=True),
     )
@@ -428,7 +455,7 @@
 def parent_kernel(n, m, groups, bulks, reach, route, masked, out, PV, TP, RS, SB, RB, XH, XL, EH, EL,
                   scatter_send, scatter_come, gather_send, gather_come, spread_send, spread_come, arrive, *more):
     sems, scratch = more[:4], more[4:]
-    T, Lh, Ll, U, E, Eh, El = scratch
+    T, Lh, Ll, U, E, ES, LS = scratch
     wide, full = n // 256, n // 128
     me, here = lax.axis_index("front"), lax.axis_index("bulk")
     meet((("front", groups), ("bulk", bulks)))
@@ -529,8 +556,8 @@
     def stage(p, _):
         chol_stage(p, n, 0, lambda kk, r: PV[kk, r, :], None, *scratch, before=before,
                    after_factor=lambda p: rows.ahead(2 * p, wide, first), before_rest=before_rest)
-        EH[p] = Eh[...]
-        EL[p] = El[...]
+        EH[p] = ES[0:128, 0:128]
+        EL[p] = ES[128:256, 0:128]
         mine = T[dynamic(me, m), dynamic(p % 2, 128)]
         out[:, dynamic(p, 128)] = jnp.where(p * 128 < (me + 1) * m, mine, 0.0)
         rows.ahead(2 * p + 1, wide, first)

time: 283 us -> 267 us (0.943)
  Pallas kernels: 274 us -> 260 us
    pallas_call x1, Pallas kernels: 186 us -> 176 us  [on_device(): child_call(pivot_count, row_count, parent_count, front_groups, 4)]
    pallas_call x1, Pallas kernels: 87.5 us -> 83.7 us  [on_device(): parent_call(pivots, parent_count, front_groups, lax.axis_size('bulk'))]
where the time goes in v4:
time: 267 us
  Pallas kernels  260 us (97%)
  local copies, waits for them, and re-layouts  5.69 us (2%)
    pallas_call x1, Pallas kernels, on_device(): child_call(pivot_count, row_count, parent_count, front_groups, 4)  176 us
    pallas_call x1, Pallas kernels, on_device(): parent_call(pivots, parent_count, front_groups, lax.axis_size('bulk'))  83.7 us

profile of v4, /device:TPU:1, one launch (start us, length us, event | category | flops | bytes accessed | tf_op | source)
XLA Modules:
  0.0 266.9 jit_solution(16826563946936461051)
XLA Ops:
  0.6 0.0 copy-start.4
  0.7 0.0 copy-start.5
  0.7 0.6 copy-done.5
  1.3 0.0 copy-start.3
  1.3 0.0 copy-done.4
  1.4 0.2 fusion.1
  1.6 0.6 slice.4.hit_ref
  2.2 0.1 broadcast_in_dim.15
  2.3 0.0 copy-done.3
  2.4 0.1 bitcast_multiply_fusion.masked
  2.4 176.4 %shard_map.76 = (f32[128,2048]{1,0:T(8,128)}, f32[128,2048]{1,0:T(8,128)}, f32[128,1024]{1,0:T(8,128)}) custom-call(f32[128,2048]{1,0:T(8,128)} %bitcast.10, f32[128,2048]{1,0:T(8,128)} %bitcast.11, bf16[64,128]{1,0:T(8,128)(2,1)} %slice.4.hit_ref), custom_call_target="tpu_custom_call" | custom-call | tf_op jit(solution)/shard_map/pallas_call | solution.py:637
  178.8 0.0 copy-start
  178.8 1.0 copy-done
  179.9 0.0 copy-start.2
  179.9 83.7 %shard_map.77 = f32[64,1024]{1,0:T(8,128)S(1)} custom-call(f32[128,1024]{1,0:T(8,128)S(1)} %copy-done, bf16[512,128]{1,0:T(8,128)(2,1)S(1)} %fusion.route, f32[64,1024]{1,0:T(8,128)S(1)} %bitcast_multiply_fusion.masked), custom_call_target="tpu_custom_call" | custom-call | tf_op jit(solution)/shard_map/pallas_call | solution.py:646
  263.6 0.0 copy-done.2
  263.6 0.0 copy-start.1
  263.6 1.0 copy.15
  264.6 0.6 copy-done.1
  265.2 1.0 copy.16
  266.2 0.7 copy.17
  (3 shorter events, 0.1 us)
Async XLA Ops:
  0.6 0.7 copy-start.4
  0.7 0.7 copy-start.5
  1.3 1.0 copy-start.3
  178.8 1.0 copy-start
  179.9 83.7 %copy-start.2 = (f32[128,2048]{1,0:T(8,128)S(1)}, f32[128,2048]{1,0:T(8,128)}, u32[]{:S(2)}) copy-start(f32[128,2048]{1,0:T(8,128)} %get-tuple-element.6) | copy-start | bytes 3145732
  263.6 1.6 copy-start.1

commit v5 on v4

--- a/solution.py
+++ b/solution.py
@@ -49,9 +49,11 @@
             e = jnp.where(sub == j, u[j], e)
         store_e(b, jnp.where(lane < base + sb, e, 0.0))
         d = jnp.zeros((sb, n), jnp.float32)
-        for j in range(sb):
-            for c in range(j, sb):
-                d = jnp.where((sub == j) & (lane == base + c), F[c, j], d)
+        for c in range(sb):
+            col = F[c, 0]
+            for j in range(1, c + 1):
+                col = jnp.where(sub == j, F[c, j], col)
+            d = jnp.where((lane == base + c) & (sub <= c), col, d)
         store_u(b, jnp.where(inblk, d, jnp.where(lane < base, 0.0, e)))
         for v in range(b + 1, nb):
             C = []
@@ -293,8 +295,8 @@
 
     def prologue(self, first):
         first(0)
+        first(1)
         self.start(1, 0)
-        first(1)
         self.start(2, 0)
         self.start(1, 1)
         first(2)
@@ -320,7 +322,7 @@
             def _():
                 first(j + 4)
 
-        @pl.when((s % 3 == 1) & (j + 1 < wide))
+        @pl.when((s % 3 == 2) & (j + 1 < wide))
         def _():
             self.start(3, j + 1)
 
@@ -411,7 +413,8 @@
         def _():
             cols = dynamic(k, 256)
             nn = functools.partial(jnp.dot, preferred_element_type=F32)
-            LG[k, dynamic(me, land), :] = nn(hit_ref[...], Lh[n:n + m, cols]) + nn(hit_ref[...], Ll[n:n + m, cols])
+            hits = hit_ref[0:land, :]
+            LG[k, dynamic(me, land), :] = nn(hits, Lh[n:n + m, cols]) + nn(hits, Ll[n:n + m, cols])
         rows.ahead(2 * p + 1, wide, first)
         catch_up(p, 12, 4, 2, lambda k: lands.start(2, k))
         catch_up(p, 14, 7, 4, land_use)
@@ -635,7 +638,7 @@
     spread_rows = lax.axis_size("bulk") * parent_count
     routing = (jnp.arange(spread_rows)[:, None] == slot_index[None, :]).astype(BF)
     lower_rows, coupling, reached = child_call(pivot_count, row_count, parent_count, front_groups, 4)(
-        own_rows, child_coupling[0], routing[:parent_count]
+        own_rows, child_coupling[0], routing
     )
     device_index = lax.axis_index("bulk") * front_groups + front_index
     first_row = device_index * parent_count

time: 267 us -> 269 us (level)
    pallas_call x1, Pallas kernels: 176 us -> 172 us  [on_device(): child_call(pivot_count, row_count, parent_count, front_groups, 4)]
    pallas_call x1, Pallas kernels: 83.7 us -> 86.5 us  [on_device(): parent_call(pivots, parent_count, front_groups, lax.axis_size('bulk'))]
where the time goes in v5:
time: 269 us; the launch traced here: 266 us
  Pallas kernels  259 us (96%)
  local copies, waits for them, and re-layouts  4.44 us (2%)
    pallas_call x1, Pallas kernels, on_device(): child_call(pivot_count, row_count, parent_count, front_groups, 4)  172 us
    pallas_call x1, Pallas kernels, on_device(): parent_call(pivots, parent_count, front_groups, lax.axis_size('bulk'))  86.5 us

profile of v5, /device:TPU:1, one launch (start us, length us, event | category | flops | bytes accessed | tf_op | source)
XLA Modules:
  0.0 266.5 jit_solution(9782877132968341082)
XLA Ops:
  0.6 0.0 copy-start.4
  0.7 0.7 fusion.5
  1.4 0.9 fusion.1
  2.3 0.7 fusion.hit_ref.route
  3.0 0.1 broadcast_in_dim.15
  3.1 0.0 copy-done.4
  3.1 0.1 bitcast_multiply_fusion.masked
  3.2 0.0 copy-start
  3.2 172.5 %shard_map.76 = (f32[128,2048]{1,0:T(8,128)}, f32[128,2048]{1,0:T(8,128)}, f32[128,1024]{1,0:T(8,128)}) custom-call(f32[128,2048]{1,0:T(8,128)} %bitcast.10, f32[128,2048]{1,0:T(8,128)} %bitcast.11, bf16[512,128]{1,0:T(8,128)(2,1)} %fusion.hit_ref.route), custom_call_target="tpu_custom_call" | custom-call | tf_op jit(solution)/shard_map/pallas_call | solution.py:640
  175.7 0.0 copy-done
  175.7 0.0 copy-start.1
  175.7 1.0 copy-done.1
  176.7 0.0 copy-start.3
  176.7 86.5 %shard_map.77 = f32[64,1024]{1,0:T(8,128)S(1)} custom-call(f32[128,1024]{1,0:T(8,128)S(1)} %copy-done.1, bf16[512,128]{1,0:T(8,128)(2,1)S(1)} %copy-done, f32[64,1024]{1,0:T(8,128)S(1)} %bitcast_multiply_fusion.masked), custom_call_target="tpu_custom_call" | custom-call | tf_op jit(solution)/shard_map/pallas_call | solution.py:649
  263.2 0.0 copy-done.3
  263.2 0.0 copy-start.2
  263.2 1.0 copy.15
  264.2 0.6 copy-done.2
  264.8 1.0 copy.16
  265.8 0.7 copy.17
  (1 shorter events, 0.0 us)
Async XLA Ops:
  0.6 2.5 copy-start.4
  3.2 172.5 %copy-start = (bf16[512,128]{1,0:T(8,128)(2,1)S(1)}, bf16[512,128]{1,0:T(8,128)(2,1)}, u32[]{:S(2)}) copy-start(bf16[512,128]{1,0:T(8,128)(2,1)} %fusion.hit_ref.route) | copy-start | bytes 393220
  175.7 1.0 copy-start.1
  176.7 86.5 %copy-start.3 = (f32[128,2048]{1,0:T(8,128)S(1)}, f32[128,2048]{1,0:T(8,128)}, u32[]{:S(2)}) copy-start(f32[128,2048]{1,0:T(8,128)} %get-tuple-element.6) | copy-start | bytes 3145732
  263.2 1.6 copy-start.2

commit v6 on v4

--- a/solution.py
+++ b/solution.py
@@ -529,13 +529,13 @@
     def first(k):
         rows.start(0, k)
     first(0)
+    first(1)
+    rows.start(1, 0)
+    rows.start(2, 0)
     for d in range(1, bulks):
         @pl.when(other(d) != 0)
         def _():
             spread(d).start()
-    rows.start(1, 0)
-    first(1)
-    rows.start(2, 0)
     rows.start(1, 1)
     first(2)
     rows.start(3, 0)

time: 267 us -> 268 us (level)
  no operation moved by 1% of the time
where the time goes in v6:
time: 268 us; the launch traced here: 267 us
  Pallas kernels  260 us (97%)
  local copies, waits for them, and re-layouts  5.69 us (2%)
    pallas_call x1, Pallas kernels, on_device(): child_call(pivot_count, row_count, parent_count, front_groups, 4)  176 us
    pallas_call x1, Pallas kernels, on_device(): parent_call(pivots, parent_count, front_groups, lax.axis_size('bulk'))  83.6 us

profile of v6, /device:TPU:1, one launch (start us, length us, event | category | flops | bytes accessed | tf_op | source)
XLA Modules:
  0.0 266.7 jit_solution(4035561747485566789)
XLA Ops:
  0.6 0.0 copy-start.4
  0.7 0.0 copy-start.5
  0.7 0.6 copy-done.5
  1.3 0.0 copy-start.3
  1.3 0.0 copy-done.4
  1.4 0.2 fusion.1
  1.6 0.6 slice.4.hit_ref
  2.2 0.1 broadcast_in_dim.15
  2.3 0.0 copy-done.3
  2.4 0.1 bitcast_multiply_fusion.masked
  2.4 176.4 %shard_map.76 = (f32[128,2048]{1,0:T(8,128)}, f32[128,2048]{1,0:T(8,128)}, f32[128,1024]{1,0:T(8,128)}) custom-call(f32[128,2048]{1,0:T(8,128)} %bitcast.10, f32[128,2048]{1,0:T(8,128)} %bitcast.11, bf16[64,128]{1,0:T(8,128)(2,1)} %slice.4.hit_ref), custom_call_target="tpu_custom_call" | custom-call | tf_op jit(solution)/shard_map/pallas_call | solution.py:637
  178.8 0.0 copy-start
  178.8 1.0 copy-done
  179.9 0.0 copy-start.2
  179.9 83.6 %shard_map.77 = f32[64,1024]{1,0:T(8,128)S(1)} custom-call(f32[128,1024]{1,0:T(8,128)S(1)} %copy-done, bf16[512,128]{1,0:T(8,128)(2,1)S(1)} %fusion.route, f32[64,1024]{1,0:T(8,128)S(1)} %bitcast_multiply_fusion.masked), custom_call_target="tpu_custom_call" | custom-call | tf_op jit(solution)/shard_map/pallas_call | solution.py:646
  263.5 0.0 copy-done.2
  263.5 0.0 copy-start.1
  263.5 1.0 copy.15
  264.5 0.6 copy-done.1
  265.1 1.0 copy.16
  266.0 0.7 copy.17
  (3 shorter events, 0.1 us)
Async XLA Ops:
  0.6 0.7 copy-start.4
  0.7 0.7 copy-start.5
  1.3 1.0 copy-start.3
  178.8 1.0 copy-start
  179.9 83.6 %copy-start.2 = (f32[128,2048]{1,0:T(8,128)S(1)}, f32[128,2048]{1,0:T(8,128)}, u32[]{:S(2)}) copy-start(f32[128,2048]{1,0:T(8,128)} %get-tuple-element.6) | copy-start | bytes 3145732
  263.5 1.6 copy-start.1
